TPU v7x, 32 devices: a whole 2x2x4 slice. The times are simulated.
32 devices in a mesh: dp: 4 (over y, core), ctx: 8 (over z, x).
Axes of the slice: x: 2, y: 2, z: 4, core: 2. Of those that a mesh axis runs over, the one named last changes fastest.
Arguments:
- inputs: float32 [4, 1024, 576], P('dp', 'ctx'), may hold values from -6 to 6
- segment_ids: int32 [4, 1024], P('dp', 'ctx'), may hold values from 0 to 2, never falling along the last dimension, each value on 1 to 512 neighbouring positions
- gain_attn: float32 [576], replicated, may hold values from 0.5 to 1.5
- gain_ffn: float32 [576], replicated, may hold values from 0.5 to 1.5
- w_query: bfloat16 [331776], P(('dp', 'ctx')), may hold values from -0.25 to 0.25
- w_key: bfloat16 [110592], P(('dp', 'ctx')), may hold values from -0.25 to 0.25
- w_value: bfloat16 [110592], P(('dp', 'ctx')), may hold values from -0.25 to 0.25
- w_out: bfloat16 [331776], P(('dp', 'ctx')), may hold values from -4 to 4
- w_gate: bfloat16 [884736], P(('dp', 'ctx')), may hold values from -0.25 to 0.25
- w_up: bfloat16 [884736], P(('dp', 'ctx')), may hold values from -0.25 to 0.25
- w_down: bfloat16 [884736], P(('dp', 'ctx')), may hold values from -0.15625 to 0.15625
- cotangent: float32 [4, 1024, 576], P('dp', 'ctx'), may hold values from -6 to 6
Outputs:
- outputs: float32 [4, 1024, 576], P('dp', 'ctx')
- grad_inputs: float32 [4, 1024, 576], P('dp', 'ctx')
- grad_gain_attn: float32 [576], replicated
- grad_gain_ffn: float32 [576], replicated
- grad_w_query: float32 [331776], P(('dp', 'ctx'))
- grad_w_key: float32 [110592], P(('dp', 'ctx'))
- grad_w_value: float32 [110592], P(('dp', 'ctx'))
- grad_w_out: float32 [331776], P(('dp', 'ctx'))
- grad_w_gate: float32 [884736], P(('dp', 'ctx'))
- grad_w_up: float32 [884736], P(('dp', 'ctx'))
- grad_w_down: float32 [884736], P(('dp', 'ctx'))
Inputs may be any that keep to these rules, and one draw needn't show every extreme that they name: `segment_ids`: within a sequence the numbers never fall; a document is one run of equal numbers, of at most 512 positions.
All inputs are finite; a program needn't handle non-finite values.
Results may differ from a plain program's by a relative error of at most 0.02.
Values may be sent and summed in bfloat16 or wider, within the bound.
A program may use at most 128 MiB of HBM per device.

v0:
```python
import jax
import jax.numpy as jnp
from jax import lax
from jax.sharding import PartitionSpec as P

D = 576
H = 9
KV = 3
HD = 64
FF = 1536


norm_epsilon = 1e-05
rope_base = 100000.0


def matmul(left, right):
    return jnp.dot(left, right, preferred_element_type=jnp.float32)


def rope_tables(positions):
    half_size = HD // 2
    exponent = jnp.arange(half_size).astype(jnp.float32) * (2.0 / HD)
    frequency = rope_base ** (-exponent)
    angles = positions[:, None] * frequency[None, :]
    return (jnp.cos(angles), jnp.sin(angles))


def rotate(tensor, cos_table, sin_table, direction):
    half_size = HD // 2
    first_half = tensor[..., :half_size]
    second_half = tensor[..., half_size:]
    cos_wide = cos_table[:, None, :]
    sin_wide = sin_table[:, None, :] * direction
    return jnp.concatenate(
        [
            first_half * cos_wide - second_half * sin_wide,
            second_half * cos_wide + first_half * sin_wide,
        ],
        axis=-1,
    )


def norm_back(grad_norm, values_in, inverse, gain):
    scaled_in = values_in * inverse
    grad_scaled = grad_norm * gain
    grad_in = inverse * (
        grad_scaled - scaled_in * jnp.mean(grad_scaled * scaled_in, axis=-1, keepdims=True)
    )
    return (grad_in, jnp.sum(grad_norm * scaled_in, axis=0))


def unpack_weights(flat):
    return (
        flat[0].reshape(D, H * HD),
        flat[1].reshape(D, KV * HD),
        flat[2].reshape(D, KV * HD),
        flat[3].reshape(H * HD, D),
        flat[4].reshape(D, FF),
        flat[5].reshape(D, FF),
        flat[6].reshape(FF, D),
    )


def on_device(
    inputs,
    segment_ids,
    gain_attn,
    gain_ffn,
    w_query,
    w_key,
    w_value,
    w_out,
    w_gate,
    w_up,
    w_down,
    cotangent,
):
    head_group = H // KV
    scale_factor = HD ** (-0.5)
    span_rows = inputs.shape[1]
    ctx_count = lax.axis_size("ctx")
    seq_rows = span_rows * ctx_count
    key_block = min(512, seq_rows)
    my_block = lax.axis_index("ctx")
    first_pos = my_block * span_rows
    query_pos = first_pos + jnp.arange(span_rows, dtype=jnp.int32)
    last_pos = first_pos + span_rows - 1
    block_count = last_pos // key_block + 1
    cos_table, sin_table = rope_tables(query_pos.astype(jnp.float32))
    grad_mats = [
        jnp.zeros((D, H * HD), jnp.float32),
        jnp.zeros((D, KV * HD), jnp.float32),
        jnp.zeros((D, KV * HD), jnp.float32),
        jnp.zeros((H * HD, D), jnp.float32),
        jnp.zeros((D, FF), jnp.float32),
        jnp.zeros((D, FF), jnp.float32),
        jnp.zeros((FF, D), jnp.float32),
    ]
    fwd_mats = unpack_weights(
        (
            lax.all_gather(w_query, ("dp", "ctx"), axis=0, tiled=True),
            lax.all_gather(w_key, ("dp", "ctx"), axis=0, tiled=True),
            lax.all_gather(w_value, ("dp", "ctx"), axis=0, tiled=True),
            lax.all_gather(w_out, ("dp", "ctx"), axis=0, tiled=True),
            lax.all_gather(w_gate, ("dp", "ctx"), axis=0, tiled=True),
            lax.all_gather(w_up, ("dp", "ctx"), axis=0, tiled=True),
            lax.all_gather(w_down, ("dp", "ctx"), axis=0, tiled=True),
        )
    )
    mat_query, mat_key, mat_value, mat_out, mat_gate, mat_up, mat_down = fwd_mats
    row_input = inputs[0]
    row_segs = segment_ids[0]
    row_cot = cotangent[0]
    inv_attn = lax.rsqrt(jnp.mean(row_input * row_input, axis=-1, keepdims=True) + norm_epsilon)
    normed_attn = (row_input * inv_attn * gain_attn).astype(jnp.bfloat16)
    queries = rotate(
        matmul(normed_attn, mat_query).reshape(span_rows, H, HD), cos_table, sin_table, 1.0
    ).astype(jnp.bfloat16)
    keys_rot = rotate(
        matmul(normed_attn, mat_key).reshape(span_rows, KV, HD), cos_table, sin_table, 1.0
    ).astype(jnp.bfloat16)
    values_own = matmul(normed_attn, mat_value).astype(jnp.bfloat16)
    packed_kv = jnp.concatenate([keys_rot.reshape(span_rows, KV * HD), values_own], axis=1)
    grouped_q = queries.reshape(span_rows, KV, head_group, HD)
    initial = (
        jnp.full((KV, head_group, span_rows), -1e30, jnp.float32),
        jnp.zeros((KV, head_group, span_rows), jnp.float32),
        jnp.zeros((KV, head_group, span_rows, HD), jnp.float32),
    )
    piece_kv = lax.all_gather(packed_kv, "ctx", axis=0, tiled=True)
    piece_segs = lax.all_gather(row_segs, "ctx", axis=0, tiled=True)
    piece_rows = piece_kv.shape[0]

    def attend_piece(current):
        running_max, running_sum, running_acc = current
        piece_keys = piece_kv[:, : KV * HD].reshape(piece_rows, KV, HD)
        piece_vals = piece_kv[:, KV * HD :].reshape(piece_rows, KV, HD)
        scores = (
            jnp.einsum("qkgd,skd->kgqs", grouped_q, piece_keys, preferred_element_type=jnp.float32)
            * scale_factor
        )
        key_pos = jnp.arange(piece_rows, dtype=jnp.int32)
        allowed = (row_segs[:, None] == piece_segs[None, :]) & (
            key_pos[None, :] <= query_pos[:, None]
        )
        scores = jnp.where(allowed[None, None], scores, -jnp.inf)
        new_max = jnp.maximum(running_max, jnp.max(scores, axis=-1))
        weights_now = jnp.exp(scores - new_max[..., None])
        new_acc = jnp.einsum(
            "kgqs,skd->kgqd",
            weights_now.astype(jnp.bfloat16),
            piece_vals,
            preferred_element_type=jnp.float32,
        )
        return (new_max, jnp.sum(weights_now, axis=-1), new_acc)

    final_max, final_sum, final_acc = lax.cond(
        jnp.int32(0) <= last_pos, attend_piece, lambda current: current, initial
    )
    log_total = final_max + jnp.log(final_sum)
    attn = (
        (final_acc / final_sum[..., None])
        .transpose(2, 0, 1, 3)
        .reshape(span_rows, H * HD)
        .astype(jnp.bfloat16)
    )
    hidden = row_input + matmul(attn, mat_out)
    inv_ffn = lax.rsqrt(jnp.mean(hidden * hidden, axis=-1, keepdims=True) + norm_epsilon)
    normed_ffn = (hidden * inv_ffn * gain_ffn).astype(jnp.bfloat16)
    gate = matmul(normed_ffn, mat_gate)
    up_proj = matmul(normed_ffn, mat_up)
    sigma = jax.nn.sigmoid(gate)
    mixed = (gate * sigma * up_proj).astype(jnp.bfloat16)
    out_rows = [hidden + matmul(mixed, mat_down)]
    bwd_mats = unpack_weights(
        (
            lax.all_gather(w_query, ("dp", "ctx"), axis=0, tiled=True),
            lax.all_gather(w_key, ("dp", "ctx"), axis=0, tiled=True),
            lax.all_gather(w_value, ("dp", "ctx"), axis=0, tiled=True),
            lax.all_gather(w_out, ("dp", "ctx"), axis=0, tiled=True),
            lax.all_gather(w_gate, ("dp", "ctx"), axis=0, tiled=True),
            lax.all_gather(w_up, ("dp", "ctx"), axis=0, tiled=True),
            lax.all_gather(w_down, ("dp", "ctx"), axis=0, tiled=True),
        )
    )
    mat_query, mat_key, mat_value, mat_out, mat_gate, mat_up, mat_down = bwd_mats
    cot_low = row_cot.astype(jnp.bfloat16)
    grad_mats[6] = matmul(mixed.T, cot_low)
    grad_mixed = matmul(cot_low, mat_down.T)
    grad_up = (grad_mixed * gate * sigma).astype(jnp.bfloat16)
    grad_gate = (grad_mixed * up_proj * sigma * (1.0 + gate * (1.0 - sigma))).astype(jnp.bfloat16)
    grad_mats[4] = matmul(normed_ffn.T, grad_gate)
    grad_mats[5] = matmul(normed_ffn.T, grad_up)
    grad_normed_ffn = matmul(grad_gate, mat_gate.T) + matmul(grad_up, mat_up.T)
    grad_res_ffn, gain_term = norm_back(grad_normed_ffn, hidden, inv_ffn, gain_ffn)
    grad_gffn = gain_term
    grad_hidden = row_cot + grad_res_ffn
    grad_hidden_low = grad_hidden.astype(jnp.bfloat16)
    grad_mats[3] = matmul(attn.T, grad_hidden_low)
    grad_attn = matmul(grad_hidden_low, mat_out.T).astype(jnp.bfloat16)
    grad_grouped = grad_attn.reshape(span_rows, KV, head_group, HD)
    delta = jnp.sum(
        grad_grouped.astype(jnp.float32)
        * attn.reshape(span_rows, KV, head_group, HD).astype(jnp.float32),
        axis=-1,
    ).transpose(1, 2, 0)
    all_kv = lax.all_gather(packed_kv, "ctx", axis=0, tiled=True)
    all_segs = lax.all_gather(row_segs, "ctx", axis=0, tiled=True)

    def key_step(block_index, state):
        grad_q_acc, key_terms = state
        first_row = block_index * key_block
        block_kv = lax.dynamic_slice_in_dim(all_kv, first_row, key_block, 0)
        block_segs = lax.dynamic_slice_in_dim(all_segs, first_row, key_block, 0)
        block_keys = block_kv[:, : KV * HD].reshape(key_block, KV, HD)
        block_vals = block_kv[:, KV * HD :].reshape(key_block, KV, HD)
        scores = (
            jnp.einsum("qkgd,skd->kgqs", grouped_q, block_keys, preferred_element_type=jnp.float32)
            * scale_factor
        )
        key_pos = first_row + jnp.arange(key_block, dtype=jnp.int32)
        allowed = (row_segs[:, None] == block_segs[None, :]) & (
            key_pos[None, :] <= query_pos[:, None]
        )
        scores = jnp.where(allowed[None, None], scores, -jnp.inf)
        probs = jnp.exp(scores - log_total[..., None])
        grad_probs = jnp.einsum(
            "qkgd,skd->kgqs", grad_grouped, block_vals, preferred_element_type=jnp.float32
        )
        grad_scores = (probs * (grad_probs - delta[..., None])).astype(jnp.bfloat16)
        grad_q_acc = (
            grad_q_acc
            + jnp.einsum(
                "kgqs,skd->qkgd", grad_scores, block_keys, preferred_element_type=jnp.float32
            )
            * scale_factor
        )
        grad_k_block = (
            jnp.einsum("kgqs,qkgd->skd", grad_scores, grouped_q, preferred_element_type=jnp.float32)
            * scale_factor
        )
        grad_v_block = jnp.einsum(
            "kgqs,qkgd->skd",
            probs.astype(jnp.bfloat16),
            grad_grouped,
            preferred_element_type=jnp.float32,
        )
        block_terms = jnp.concatenate(
            [grad_k_block.reshape(key_block, KV * HD), grad_v_block.reshape(key_block, KV * HD)],
            axis=1,
        )
        return (grad_q_acc, lax.dynamic_update_slice_in_dim(key_terms, block_terms, first_row, 0))

    start_state = (
        jnp.zeros((span_rows, KV, head_group, HD), jnp.float32),
        jnp.zeros((seq_rows, 2 * KV * HD), jnp.float32),
    )
    grad_q_rot, key_terms = lax.fori_loop(0, block_count, key_step, start_state)
    own_grads = lax.psum_scatter(key_terms, "ctx", scatter_dimension=0, tiled=True)
    grad_queries = (
        rotate(grad_q_rot.reshape(span_rows, H, HD), cos_table, sin_table, -1.0)
        .astype(jnp.bfloat16)
        .reshape(span_rows, H * HD)
    )
    grad_keys = (
        rotate(own_grads[:, : KV * HD].reshape(span_rows, KV, HD), cos_table, sin_table, -1.0)
        .astype(jnp.bfloat16)
        .reshape(span_rows, KV * HD)
    )
    grad_values = own_grads[:, KV * HD :].astype(jnp.bfloat16)
    grad_mats[0] = matmul(normed_attn.T, grad_queries)
    grad_mats[1] = matmul(normed_attn.T, grad_keys)
    grad_mats[2] = matmul(normed_attn.T, grad_values)
    grad_normed_attn = (
        matmul(grad_queries, mat_query.T)
        + matmul(grad_keys, mat_key.T)
        + matmul(grad_values, mat_value.T)
    )
    grad_res_attn, gain_term = norm_back(grad_normed_attn, row_input, inv_attn, gain_attn)
    grad_rows = [grad_hidden + grad_res_attn]
    reduced = (
        lax.psum_scatter(grad_mats[0].reshape(-1), ("dp", "ctx"), scatter_dimension=0, tiled=True),
        lax.psum_scatter(grad_mats[1].reshape(-1), ("dp", "ctx"), scatter_dimension=0, tiled=True),
        lax.psum_scatter(grad_mats[2].reshape(-1), ("dp", "ctx"), scatter_dimension=0, tiled=True),
        lax.psum_scatter(grad_mats[3].reshape(-1), ("dp", "ctx"), scatter_dimension=0, tiled=True),
        lax.psum_scatter(grad_mats[4].reshape(-1), ("dp", "ctx"), scatter_dimension=0, tiled=True),
        lax.psum_scatter(grad_mats[5].reshape(-1), ("dp", "ctx"), scatter_dimension=0, tiled=True),
        lax.psum_scatter(grad_mats[6].reshape(-1), ("dp", "ctx"), scatter_dimension=0, tiled=True),
    )
    gain_sums = lax.psum((gain_term, grad_gffn), ("dp", "ctx"))
    return (
        jnp.stack(out_rows),
        jnp.stack(grad_rows),
        gain_sums[0],
        gain_sums[1],
        reduced[0],
        reduced[1],
        reduced[2],
        reduced[3],
        reduced[4],
        reduced[5],
        reduced[6],
    )


def solution(mesh):
    return jax.shard_map(
        on_device,
        mesh=mesh,
        in_specs=(
            P("dp", "ctx", None),
            P("dp", "ctx"),
            P(),
            P(),
            P(("dp", "ctx")),
            P(("dp", "ctx")),
            P(("dp", "ctx")),
            P(("dp", "ctx")),
            P(("dp", "ctx")),
            P(("dp", "ctx")),
            P(("dp", "ctx")),
            P("dp", "ctx", None),
        ),
        out_specs=(
            P("dp", "ctx", None),
            P("dp", "ctx", None),
            P(),
            P(),
            P(("dp", "ctx")),
            P(("dp", "ctx")),
            P(("dp", "ctx")),
            P(("dp", "ctx")),
            P(("dp", "ctx")),
            P(("dp", "ctx")),
            P(("dp", "ctx")),
        ),
        check_vma=False,
    )
```

profile of v0, /device:TPU:0, one launch (start us, length us, event | category | flops | bytes accessed | tf_op | source)
XLA Modules:
  0.0 757.3 jit_solution(16299563339428927874)
XLA Ops:
  9.5 0.7 reshape.450
  10.2 73.0 %all-gather.2 = bf16[32,1,3456]{2,1,0:T(2,128)(2,1)S(1)} all-gather(bf16[1,1,3456]{2,1,0:T(2,128)(2,1)S(1)} %reshape.450), channel_id=1, replica_groups=mesh['dp'=4,'ctx'=8] {'dp','ctx'}, dimensions={0}, use_global_device_ids=true | all-gather | bytes 228096 | tf_op jit(solution)/shard_map/all_gather | solution.py:104
  83.2 1.1 fusion.25
  84.3 0.7 reshape.448
  85.0 0.8 reshape.452
  85.7 79.1 %all-gather.3 = bf16[32,1,10368]{2,1,0:T(2,128)(2,1)} all-gather(bf16[1,1,10368]{2,1,0:T(2,128)(2,1)S(1)} %reshape.452), channel_id=1, replica_groups=mesh['dp'=4,'ctx'=8] {'dp','ctx'}, dimensions={0}, use_global_device_ids=true | all-gather | bytes 684288 | tf_op jit(solution)/shard_map/all_gather | solution.py:102
  164.8 73.2 %all-gather.4 = bf16[32,1,10368]{2,1,0:T(2,128)(2,1)S(1)} all-gather(bf16[1,1,10368]{2,1,0:T(2,128)(2,1)S(1)} %reshape.454), channel_id=1, replica_groups=mesh['dp'=4,'ctx'=8] {'dp','ctx'}, dimensions={0}, use_global_device_ids=true | all-gather | bytes 684288 | tf_op jit(solution)/shard_map/all_gather | solution.py:105
  238.2 0.8 broadcast_multiply_fusion
  238.9 68.4 %all-gather.1 = bf16[32,1,3456]{2,1,0:T(2,128)(2,1)S(1)} all-gather(bf16[1,1,3456]{2,1,0:T(2,128)(2,1)S(1)} %reshape.448), channel_id=1, replica_groups=mesh['dp'=4,'ctx'=8] {'dp','ctx'}, dimensions={0}, use_global_device_ids=true | all-gather | bytes 228096 | tf_op jit(solution)/shard_map/all_gather | solution.py:103
  307.3 1.3 reduce.1
  308.6 0.9 reshape.431
  309.6 1.3 reduce
  311.1 0.9 copy.40
  311.9 5.0 reduce.2
  316.9 0.9 reshape.432
  318.2 5.2 reduce.3
  323.4 2.0 reshape.433
  325.4 16.6 %all-gather = s32[1,1024]{1,0:T(1,128)} all-gather(s32[1,128]{1,0:T(1,128)S(1)} %copy-done.38), channel_id=2, replica_groups=mesh['dp'=4,'ctx'=8] {'ctx'}, dimensions={1}, use_global_device_ids=true | all-gather | bytes 4608 | tf_op jit(solution)/shard_map/all_gather | solution.py:132
  342.0 1.2 fusion.32
  343.2 1.3 convolution_convert_fusion.1
  344.9 29.0 %all_gather.39 = bf16[1024,384]{0,1:T(8,128)(2,1)S(1)} all-gather(bf16[128,384]{0,1:T(8,128)(2,1)S(1)} %pad_maximum_fusion.2), channel_id=1, replica_groups=mesh['dp'=4,'ctx'=8] {'ctx'}, dimensions={0}, use_global_device_ids=true | all-gather | bytes 884736 | tf_op jit(solution)/shard_map/all_gather | solution.py:131
  373.9 7.3 conditional.1
  373.9 0.9 fusion.8
  374.9 0.9 fusion.4
  376.4 2.3 fusion.3
  378.6 1.9 fusion.5
  382.0 0.7 divide_convert_fusion
  383.4 3.6 reshape.434
  387.1 4.5 reshape.435
  391.6 1.4 fusion.53
  393.1 1.4 fusion.54
  394.5 4.3 reshape.436
  398.7 3.7 multiply_convert_fusion
  403.0 1.1 copy-done.1
  404.2 1.3 multiply_reduce_fusion
  406.1 0.8 multiply_reduce_fusion.3
  407.0 4.3 while.13
  407.8 0.8 dynamic_slice.9
  408.8 0.9 fusion.131
  411.3 1.2 copy-done.11
  413.1 1.7 reshape.440
  415.1 1.7 reshape.443
  416.8 1.7 fusion.56
  418.5 2.1 reshape.444
  420.6 1.7 fusion.57
  422.3 2.1 reshape.445
  424.4 3.7 fusion.49
  428.1 5.3 reshape.446
  433.4 45.3 %reduce-scatter.2.cloned.1.call-done = f32[128,384]{0,1:T(8,128)} async-done(((f32[1024,384]{0,1:T(8,128)}), f32[128,384]{0,1:T(8,128)}) %reduce-scatter.2.cloned.1.call-update) | async-done | bytes 196624 | tf_op jit(solution)/shard_map/reduce_scatter | solution.py:260
  478.7 1.0 slice.61
  480.0 1.1 reshape.441
  481.4 1.1 reshape.442
  482.5 1.5 copy-done.4
  484.0 2.6 fusion.24
  487.7 41.5 %all-reduce.7 = (f32[576]{0:T(1024)}, f32[576]{0:T(1024)}) all-reduce(f32[576]{0:T(1024)S(1)} %get-tuple-element.131, f32[576]{0:T(1024)S(1)} %copy-done.41), channel_id=1, replica_groups=mesh['dp'=4,'ctx'=8] {'dp','ctx'}, use_global_device_ids=true, to_apply=%region_13.14 | all-reduce | flops 1152 | bytes 9216 | tf_op jit(solution)/shard_map/psum | solution.py:291
  529.1 0.9 add_bitcast_fusion
  530.0 210.1 %all-reduce.11.cloned.1.call-done = (f32[331776]{0:T(1024)}, f32[110592]{0:T(1024)}, f32[110592]{0:T(1024)}, f32[331776]{0:T(1024)}, f32[884736]{0:T(1024)}, /*index=5*/f32[884736]{0:T(1024)}, f32[884736]{0:T(1024)}) async-done(((f32[331776]{0:T(1024)}, f32[110592]{0:T(1024)}, f32[110592]{0:T(1024)}, f32[331776]{0:T(1024)}, f32[884736]{0:T(1024)}, /*index=5*/f32[884736]{0:T(1024)}, f32[884736]{0:T(1024)}), ...) | async-done | bytes 14155792
  740.2 1.4 dynamic-slice.1
  741.6 1.4 dynamic-slice.2
  743.0 1.5 dynamic-slice
  744.5 1.5 dynamic-slice.3
  746.0 1.5 dynamic-slice.4
  747.5 1.5 dynamic-slice.5
  749.1 1.5 dynamic-slice.6
  (148 shorter events, 12.4 us)
Async XLA Ops:
  7.2 230.9 %copy-start.2 = (f32[1,128,576]{1,2,0:T(8,128)S(1)}, f32[1,128,576]{1,2,0:T(8,128)}, u32[]{:S(2)}) copy-start(f32[1,128,576]{1,2,0:T(8,128)} %param.16) | copy-start | bytes 884740
  7.2 157.6 %copy-start.40 = (bf16[10368]{0:T(1024)(128)(2,1)S(1)}, bf16[10368]{0:T(1024)(128)(2,1)}, u32[]{:S(2)}) copy-start(bf16[10368]{0:T(1024)(128)(2,1)} %param.23) | copy-start | bytes 62212
  7.2 230.8 %copy-start.34 = (f32[576]{0:T(1024)S(1)}, f32[576]{0:T(1024)}, u32[]{:S(2)}) copy-start(f32[576]{0:T(1024)} %param.18) | copy-start | bytes 6916
  7.2 376.2 %all-gather.9.cloned.1.call-start = ((), (), s32[]{:S(2)}) async-start(), calls=%async_computation.1 | async-start | bytes 1824768 | tf_op jit(solution)/shard_map/all_gather | solution.py:106
  7.9 379.1 %all-gather.11.cloned.1.call-start = ((), (), s32[]{:S(2)}) async-start(), calls=%async_computation.2 | async-start | bytes 1824768 | tf_op jit(solution)/shard_map/all_gather | solution.py:107
  8.7 385.8 %all-gather.13.cloned.1.call-start = ((), (), s32[]{:S(2)}) async-start(), calls=%async_computation.3 | async-start | bytes 1824768 | tf_op jit(solution)/shard_map/all_gather | solution.py:108
  9.4 469.3 %reduce-scatter.2.cloned.1.call-start = ((), (), s32[]{:S(2)}) async-start(), calls=%async_computation.4 | async-start | bytes 1769472 | tf_op jit(solution)/shard_map/reduce_scatter | solution.py:260
  84.3 223.1 %copy-start.42 = (f32[128]{0:T(128)}, f32[128]{0:T(128)S(1)}, u32[]{:S(2)}) copy-start(f32[128]{0:T(128)S(1)} %add_rsqrt_fusion.1) | copy-start | bytes 1540
  238.2 174.5 %copy-start.12 = (bf16[1,128,576]{1,2,0:T(8,128)(2,1)}, bf16[1,128,576]{1,2,0:T(8,128)(2,1)S(1)}, u32[]{:S(2)}) copy-start(bf16[1,128,576]{1,2,0:T(8,128)(2,1)S(1)} %multiply_convert_fusion.5) | copy-start | bytes 442372
  311.1 0.9 copy-start.18
  317.8 7.6 copy-start.7
  317.8 7.6 copy-start.38
  325.4 57.3 %copy-start.9 = (bf16[576,576]{1,0:T(8,128)(2,1)}, bf16[576,576]{1,0:T(8,128)(2,1)S(1)}, u32[]{:S(2)}) copy-start(bf16[576,576]{1,0:T(8,128)(2,1)S(1)} %reshape.433) | copy-start | bytes 1990660
  373.9 9.3 %copy-start.37 = (f32[576]{0:T(1024)S(1)}, f32[576]{0:T(1024)}, u32[]{:S(2)}) copy-start(f32[576]{0:T(1024)} %param.19) | copy-start | bytes 6916
  381.3 2.1 copy-start.20
  382.7 0.7 copy-start.27
  383.2 22.3 %copy-start.5 = (f32[128,576]{0,1:T(8,128)}, f32[128,576]{0,1:T(8,128)S(1)}, u32[]{:S(2)}) copy-start(f32[128,576]{0,1:T(8,128)S(1)} %get-tuple-element.187) | copy-start | bytes 884740
  383.4 15.3 %copy-start.17 = (bf16[128,576]{0,1:T(8,128)(2,1)}, bf16[128,576]{0,1:T(8,128)(2,1)S(1)}, u32[]{:S(2)}) copy-start(bf16[128,576]{0,1:T(8,128)(2,1)S(1)} %multiply_convert_fusion.4) | copy-start | bytes 442372
  391.6 1.5 copy-start
  402.4 3.1 copy-start.23
  402.4 3.1 copy-start.24
  402.4 1.8 copy-start.1
  402.4 3.1 copy-start.29
  403.0 2.6 copy-start.10
  404.2 1.9 copy-start.21
  405.5 1.6 copy-start.39
  405.7 1.1 copy-start.14
  407.0 5.5 copy-start.32
  411.3 1.2 copy-start.11
  412.5 327.6 %all-reduce.11.cloned.1.call-start = ((), (), s32[]{:S(2)}) async-start(), calls=%async_computation.5 | async-start | bytes 28311552
  412.7 2.5 copy-start.25
  412.7 2.1 copy-start.15
  412.7 2.1 copy-start.28
  428.1 51.6 %copy-start.33 = (f32[128,32]{0,1:T(8,128)S(1)}, f32[128,32]{0,1:T(8,128)}, u32[]{:S(2)}) copy-start(f32[128,32]{0,1:T(8,128)} %get-tuple-element.183) | copy-start | bytes 49156
  428.1 51.6 %copy-start.13 = (bf16[1,128,576]{1,2,0:T(8,128)(2,1)S(1)}, bf16[1,128,576]{1,2,0:T(8,128)(2,1)}, u32[]{:S(2)}) copy-start(bf16[1,128,576]{1,2,0:T(8,128)(2,1)} %copy-done.12) | copy-start | bytes 442372
  428.1 53.0 %copy-start.35 = (f32[576]{0:T(1024)S(1)}, f32[576]{0:T(1024)}, u32[]{:S(2)}) copy-start(f32[576]{0:T(1024)} %param.18) | copy-start | bytes 6916
  428.1 53.0 %copy-start.43 = (f32[128]{0:T(128)S(1)}, f32[128]{0:T(128)}, u32[]{:S(2)}) copy-start(f32[128]{0:T(128)} %copy-done.42) | copy-start | bytes 1540
  433.4 47.7 %copy-start.3 = (f32[1,128,576]{1,2,0:T(8,128)S(1)}, f32[1,128,576]{1,2,0:T(8,128)}, u32[]{:S(2)}) copy-start(f32[1,128,576]{1,2,0:T(8,128)} %param.16) | copy-start | bytes 884740
  478.7 2.4 copy-start.30
  482.5 1.5 copy-start.4
  482.5 1.6 copy-start.6
  482.5 4.1 copy-start.8
  482.5 4.1 copy-start.26
  484.0 3.0 copy-start.19
  484.0 3.2 copy-start.22
  484.0 3.2 copy-start.31
  484.0 3.2 copy-start.36
  484.0 3.2 copy-start.44
  486.6 1.0 copy-start.41
  486.6 42.5 %copy-start.16 = (f32[128,576]{0,1:T(8,128)S(1)}, f32[128,576]{0,1:T(8,128)}, u32[]{:S(2)}) copy-start(f32[128,576]{0,1:T(8,128)} %copy-done.14) | copy-start | bytes 884740
Sparse Core Ops, SparseCore 0:
  10.9 59.5 all-gather.8
  73.3 56.3 all-gather.10
  132.6 58.2 all-gather.12
  412.6 66.0 reduce-scatter.1
  486.1 253.9 all-reduce.10
where the time goes:
time: 772 us; the launch traced here: 757 us
  blocking collectives  381 us (49%)
  waiting for transfers between devices  258 us (33%)
  local copies, waits for them, and re-layouts  52.1 us (7%)
  matrix products  29.6 us (4%)
  other arithmetic  22.2 us (3%)
  between operations  14.7 us (2%)
    unnamed x6, waiting for transfers between devices  212 us
    all_gather x1, blocking collectives, on_device(): lax.all_gather(w_query, ('dp', 'ctx'), axis=0, tiled=True)  79.1 us
    all_gather x1, blocking collectives, on_device(): lax.all_gather(w_out, ('dp', 'ctx'), axis=0, tiled=True)  73.2 us
    all_gather x1, blocking collectives, on_device(): lax.all_gather(w_value, ('dp', 'ctx'), axis=0, tiled=True)  73 us
    all_gather x1, blocking collectives, on_device(): lax.all_gather(w_key, ('dp', 'ctx'), axis=0, tiled=True)  68.4 us
    reduce_scatter x1, waiting for transfers between devices, on_device(): lax.psum_scatter(key_terms, 'ctx', scatter_dimension=0, tiled=True)  45.3 us
    psum x1, blocking collectives, on_device(): gain_sums = lax.psum((gain_term, grad_gffn), ('dp', 'ctx'))  41.5 us
    all_gather x1, blocking collectives, on_device(): piece_kv = lax.all_gather(packed_kv, 'ctx', axis=0, tiled=True)  29 us
  transfers between devices with their start and end apart: 5, of which 2 were waited for; matrix products, arithmetic and copies ran while one was open for 9% of the time, Pallas kernels for 0%

commit v1 on v0

v1 whole, which is shorter than its diff:
```python
import jax
import jax.numpy as jnp
from jax import lax
from jax.experimental import pallas as pl
from jax.experimental.pallas import tpu as pltpu
from jax.sharding import PartitionSpec as P

D = 576
H = 9
KV = 3
HD = 64
FF = 1536


norm_epsilon = 1e-05
rope_base = 100000.0


def matmul(left, right):
    return jnp.dot(left, right, preferred_element_type=jnp.float32)


def rope_tables(positions):
    half_size = HD // 2
    exponent = jnp.arange(half_size).astype(jnp.float32) * (2.0 / HD)
    frequency = rope_base ** (-exponent)
    angles = positions[:, None] * frequency[None, :]
    return (jnp.cos(angles), jnp.sin(angles))


def rotate(tensor, cos_table, sin_table, direction):
    half_size = HD // 2
    first_half = tensor[..., :half_size]
    second_half = tensor[..., half_size:]
    cos_wide = cos_table[:, None, :]
    sin_wide = sin_table[:, None, :] * direction
    return jnp.concatenate(
        [
            first_half * cos_wide - second_half * sin_wide,
            second_half * cos_wide + first_half * sin_wide,
        ],
        axis=-1,
    )


def norm_back(grad_norm, values_in, inverse, gain):
    scaled_in = values_in * inverse
    grad_scaled = grad_norm * gain
    grad_in = inverse * (
        grad_scaled - scaled_in * jnp.mean(grad_scaled * scaled_in, axis=-1, keepdims=True)
    )
    return (grad_in, jnp.sum(grad_norm * scaled_in, axis=0))


def exchange(collective_id, *items):
    arrays = [array for array, _, _ in items]
    total = len(items)
    axes = sorted({axis for _, axis, _ in items})
    counts = {axis: lax.axis_size(axis) for axis in axes}
    most = max(counts.values())

    def kernel(*refs):
        sources, targets = refs[:total], refs[total : 2 * total]
        send_sem, recv_sem, own_sem = refs[2 * total :]
        place = {axis: lax.axis_index(axis) for axis in axes}

        def piece(index, peer):
            return sources[index] if items[index][2] else sources[index].at[peer]

        def partner(axis, step):
            return lax.rem(place[axis] + step, counts[axis])

        barrier = pltpu.get_barrier_semaphore()
        for axis in axes:
            for step in range(1, counts[axis]):
                pl.semaphore_signal(
                    barrier,
                    inc=1,
                    device_id={axis: partner(axis, step)},
                    device_id_type=pl.DeviceIdType.MESH,
                )
        started = []
        for index, (_, axis, _) in enumerate(items):
            me = place[axis]
            copy = pltpu.make_async_copy(piece(index, me), targets[index].at[me], own_sem.at[index])
            copy.start()
            started.append(copy)
        pl.semaphore_wait(barrier, sum(counts[axis] - 1 for axis in axes))
        for step in range(1, most):
            for index, (_, axis, _) in enumerate(items):
                if step >= counts[axis]:
                    continue
                peer = partner(axis, step)
                copy = pltpu.make_async_remote_copy(
                    src_ref=piece(index, peer),
                    dst_ref=targets[index].at[place[axis]],
                    send_sem=send_sem.at[index, step],
                    recv_sem=recv_sem.at[index, step],
                    device_id={axis: peer},
                    device_id_type=pl.DeviceIdType.MESH,
                )
                copy.start()
                started.append(copy)
        for copy in started:
            copy.wait()

    return pl.pallas_call(
        kernel,
        out_shape=[
            jax.ShapeDtypeStruct(
                (counts[axis],) + array.shape if whole else array.shape, array.dtype
            )
            for array, axis, whole in items
        ],
        in_specs=[pl.BlockSpec(memory_space=pl.ANY)] * total,
        out_specs=[pl.BlockSpec(memory_space=pl.ANY)] * total,
        scratch_shapes=[
            pltpu.SemaphoreType.DMA((total, most)),
            pltpu.SemaphoreType.DMA((total, most)),
            pltpu.SemaphoreType.DMA((total,)),
        ],
        compiler_params=pltpu.CompilerParams(collective_id=collective_id, has_side_effects=True),
    )(*arrays)


def pack(flat):
    lengths = [w.shape[0] for w in flat]
    if all(length % LANES == 0 for length in lengths):
        return jnp.concatenate([w.reshape(-1, LANES) for w in flat], axis=0)
    return jnp.concatenate(flat).reshape(1, -1)


def unpack(got, lengths, widths):
    out = []
    start = 0
    lanes = got.shape[-1] if got.shape[1] > 1 else 1
    rows_of = got if got.shape[1] > 1 else got.reshape(got.shape[0], -1)
    for length, width in zip(lengths, widths):
        step = length // lanes
        out.append(rows_of[:, start : start + step].reshape(-1, width))
        start += step
    return out


def pack_grads(slabs, count):
    sizes = [slab.size // count for slab in slabs]
    if all(size % LANES == 0 for size in sizes):
        return jnp.concatenate([slab.reshape(count, -1, LANES) for slab in slabs], axis=1)
    return jnp.concatenate([slab.reshape(count, 1, -1) for slab in slabs], axis=2)


def unpack_grads(own, lengths):
    out = []
    start = 0
    lanes = own.shape[-1] if own.shape[0] > 1 else 1
    rows_of = own if own.shape[0] > 1 else own.reshape(-1)
    for length in lengths:
        step = length // lanes
        out.append(rows_of[start : start + step].reshape(-1))
        start += step
    return out


def total_of(pieces):
    return jnp.sum(pieces.astype(jnp.float32), axis=0)


LANES = 128
low = jnp.bfloat16


def on_device(
    inputs,
    segment_ids,
    gain_attn,
    gain_ffn,
    w_query,
    w_key,
    w_value,
    w_out,
    w_gate,
    w_up,
    w_down,
    cotangent,
):
    head_group = H // KV
    scale_factor = HD ** (-0.5)
    span_rows = inputs.shape[1]
    dp_count = lax.axis_size("dp")
    ctx_count = lax.axis_size("ctx")
    seq_rows = span_rows * ctx_count
    key_block = min(1024, seq_rows)
    my_block = lax.axis_index("ctx")
    first_pos = my_block * span_rows
    query_pos = first_pos + jnp.arange(span_rows, dtype=jnp.int32)
    cos_table, sin_table = rope_tables(query_pos.astype(jnp.float32))
    row_input = inputs[0]
    row_segs = segment_ids[0]
    row_cot = cotangent[0]
    cot_low = row_cot.astype(low)

    attn_flat = (w_query, w_key, w_value, w_out)
    attn_lengths = [w.shape[0] for w in attn_flat]
    got_attn, got_segs, all_cot = exchange(
        1, (pack(attn_flat), "ctx", True), (segment_ids, "ctx", True), (cot_low, "dp", True)
    )
    all_cot = all_cot.reshape(-1, D)
    all_segs = got_segs.reshape(seq_rows)
    slabs = unpack(got_attn, attn_lengths, (H * HD, KV * HD, KV * HD, D))
    mat_qkv, mat_out, got_gate_up = exchange(
        2,
        (jnp.concatenate(slabs[:3], axis=1), "dp", True),
        (slabs[3], "dp", True),
        (pack((w_gate, w_up)), "ctx", True),
    )
    mat_qkv = mat_qkv.reshape(D, -1)
    mat_out = mat_out.reshape(H * HD, D)
    ff_part = FF // dp_count
    d_part = D // dp_count
    gate_up = jnp.concatenate(
        [
            slab.reshape(d_part, dp_count, ff_part)
            for slab in unpack(got_gate_up, (w_gate.shape[0], w_up.shape[0]), (FF, FF))
        ],
        axis=2,
    ).transpose(1, 0, 2)

    inv_attn = lax.rsqrt(jnp.mean(row_input * row_input, axis=-1, keepdims=True) + norm_epsilon)
    normed_attn = (row_input * inv_attn * gain_attn).astype(low)
    qkv = matmul(normed_attn, mat_qkv)
    turned = rotate(
        qkv[:, : (H + KV) * HD].reshape(span_rows, H + KV, HD), cos_table, sin_table, 1.0
    ).astype(low)
    grouped_q = turned[:, :H].reshape(span_rows, KV, head_group, HD)
    packed_kv = jnp.concatenate(
        [turned[:, H:].reshape(span_rows, KV * HD), qkv[:, (H + KV) * HD :].astype(low)], axis=1
    )
    all_kv, mat_gu = exchange(3, (packed_kv, "ctx", True), (gate_up, "dp", False))
    mat_gu = mat_gu.reshape(D, 2 * ff_part)
    all_kv = all_kv.reshape(seq_rows, 2 * KV * HD)
    all_keys = all_kv[:, : KV * HD].reshape(seq_rows, KV, HD)
    all_vals = all_kv[:, KV * HD :].reshape(seq_rows, KV, HD)

    def masked_scores(first_row, rows):
        block_keys = all_keys[first_row : first_row + rows]
        scores = (
            jnp.einsum("qkgd,skd->kgqs", grouped_q, block_keys, preferred_element_type=jnp.float32)
            * scale_factor
        )
        key_pos = first_row + jnp.arange(rows, dtype=jnp.int32)
        allowed = (row_segs[:, None] == all_segs[None, first_row : first_row + rows]) & (
            key_pos[None, :] <= query_pos[:, None]
        )
        return jnp.where(allowed[None, None], scores, -jnp.inf)

    scores = masked_scores(0, seq_rows)
    final_max = jnp.max(scores, axis=-1)
    weights_now = jnp.exp(scores - final_max[..., None])
    final_sum = jnp.sum(weights_now, axis=-1)
    final_acc = jnp.einsum(
        "kgqs,skd->kgqd", weights_now.astype(low), all_vals, preferred_element_type=jnp.float32
    )
    log_total = final_max + jnp.log(final_sum)
    attn = (
        (final_acc / final_sum[..., None])
        .transpose(2, 0, 1, 3)
        .reshape(span_rows, H * HD)
        .astype(low)
    )
    hidden = row_input + matmul(attn, mat_out)
    inv_ffn = lax.rsqrt(jnp.mean(hidden * hidden, axis=-1, keepdims=True) + norm_epsilon)
    normed_ffn = (hidden * inv_ffn * gain_ffn).astype(low)

    all_normed, got_down = exchange(
        4, (normed_ffn, "dp", True), (pack((w_down,)), "ctx", True)
    )
    (mat_down,) = unpack(got_down, (w_down.shape[0],), (D,))
    all_normed = all_normed.reshape(-1, D)
    gate_up_act = matmul(all_normed, mat_gu)
    gate = gate_up_act[:, :ff_part]
    up_proj = gate_up_act[:, ff_part:]
    sigma = jax.nn.sigmoid(gate)
    mixed = (gate * sigma * up_proj).astype(low)
    part_out = matmul(mixed, mat_down).astype(low).reshape(dp_count, span_rows, D)
    grad_mixed = matmul(all_cot, mat_down.T)
    grad_up = (grad_mixed * gate * sigma).astype(low)
    grad_gate = (grad_mixed * up_proj * sigma * (1.0 + gate * (1.0 - sigma))).astype(low)
    grad_gu_act = jnp.concatenate([grad_gate, grad_up], axis=1)
    part_normed = matmul(grad_gu_act, mat_gu.T).astype(low).reshape(dp_count, span_rows, D)
    grad_down = matmul(mixed.T, all_cot).astype(low)
    grad_gu = matmul(all_normed.T, grad_gu_act).astype(low).reshape(dp_count, d_part, -1)
    got_normed, got_down_grad = exchange(
        5, (part_normed, "dp", False), (pack_grads((grad_down,), ctx_count), "ctx", False)
    )
    grad_normed_ffn = total_of(got_normed)

    grad_res_ffn, grad_gffn = norm_back(grad_normed_ffn, hidden, inv_ffn, gain_ffn)
    grad_hidden = row_cot + grad_res_ffn
    grad_hidden_low = grad_hidden.astype(low)
    grad_out = matmul(attn.T, grad_hidden_low)
    grad_attn = matmul(grad_hidden_low, mat_out.T).astype(low)
    grad_grouped = grad_attn.reshape(span_rows, KV, head_group, HD)
    delta = jnp.sum(
        grad_grouped.astype(jnp.float32)
        * attn.reshape(span_rows, KV, head_group, HD).astype(jnp.float32),
        axis=-1,
    ).transpose(1, 2, 0)

    grad_q_rot = 0.0
    key_terms = []
    for first_row in range(0, seq_rows, key_block):
        block_keys = all_keys[first_row : first_row + key_block]
        block_vals = all_vals[first_row : first_row + key_block]
        probs = jnp.exp(masked_scores(first_row, key_block) - log_total[..., None])
        grad_probs = jnp.einsum(
            "qkgd,skd->kgqs", grad_grouped, block_vals, preferred_element_type=jnp.float32
        )
        grad_scores = (probs * (grad_probs - delta[..., None])).astype(low)
        grad_q_rot = (
            grad_q_rot
            + jnp.einsum(
                "kgqs,skd->qkgd", grad_scores, block_keys, preferred_element_type=jnp.float32
            )
            * scale_factor
        )
        grad_k_block = (
            jnp.einsum("kgqs,qkgd->skd", grad_scores, grouped_q, preferred_element_type=jnp.float32)
            * scale_factor
        )
        grad_v_block = jnp.einsum(
            "kgqs,qkgd->skd", probs.astype(low), grad_grouped, preferred_element_type=jnp.float32
        )
        key_terms.append(
            jnp.concatenate(
                [
                    grad_k_block.reshape(key_block, KV * HD),
                    grad_v_block.reshape(key_block, KV * HD),
                ],
                axis=1,
            ).astype(low)
        )
    key_terms = jnp.concatenate(key_terms, axis=0).reshape(ctx_count, span_rows, 2 * KV * HD)
    got_terms, got_out, got_gu, got_out_grad = exchange(
        6,
        (key_terms, "ctx", False),
        (part_out, "dp", False),
        (grad_gu, "dp", False),
        (grad_out.astype(low).reshape(dp_count, H * HD // dp_count, D), "dp", False),
    )
    out_rows = hidden + total_of(got_out)
    slab_gate = got_gu[:, :, :ff_part].transpose(1, 0, 2).reshape(d_part, FF)
    slab_up = got_gu[:, :, ff_part:].transpose(1, 0, 2).reshape(d_part, FF)
    slab_out = total_of(got_out_grad).astype(low)
    own_grads = total_of(got_terms)
    grad_qk = rotate(
        jnp.concatenate(
            [
                grad_q_rot.reshape(span_rows, H, HD),
                own_grads[:, : KV * HD].reshape(span_rows, KV, HD),
            ],
            axis=1,
        ),
        cos_table,
        sin_table,
        -1.0,
    )
    grad_qkv = jnp.concatenate(
        [grad_qk.reshape(span_rows, (H + KV) * HD).astype(low), own_grads[:, KV * HD :].astype(low)],
        axis=1,
    )
    grad_mat_qkv = matmul(normed_attn.T, grad_qkv)
    grad_normed_attn = matmul(grad_qkv, mat_qkv.T)
    grad_res_attn, grad_gattn = norm_back(grad_normed_attn, row_input, inv_attn, gain_attn)
    grad_rows = grad_hidden + grad_res_attn

    gain_terms = jnp.stack([grad_gattn, grad_gffn])
    got_gains, got_qkv, got_gu_grad = exchange(
        7,
        (gain_terms, "dp", True),
        (grad_mat_qkv.astype(low).reshape(dp_count, d_part, -1), "dp", False),
        (pack_grads((slab_gate, slab_up), ctx_count), "ctx", False),
    )
    slab_qkv = total_of(got_qkv).astype(low)
    attn_slabs = (
        slab_qkv[:, : H * HD],
        slab_qkv[:, H * HD : (H + KV) * HD],
        slab_qkv[:, (H + KV) * HD :],
        slab_out,
    )
    got_gains, got_attn_grad = exchange(
        8,
        (total_of(got_gains), "ctx", True),
        (pack_grads(attn_slabs, ctx_count), "ctx", False),
    )
    gains = total_of(got_gains)
    reduced = (
        unpack_grads(total_of(got_attn_grad), attn_lengths)
        + unpack_grads(total_of(got_gu_grad), (w_gate.shape[0], w_up.shape[0]))
        + unpack_grads(total_of(got_down_grad), (w_down.shape[0],))
    )
    return (out_rows[None], grad_rows[None], gains[0], gains[1], *reduced)


def solution(mesh):
    return jax.shard_map(
        on_device,
        mesh=mesh,
        in_specs=(
            P("dp", "ctx", None),
            P("dp", "ctx"),
            P(),
            P(),
            P(("dp", "ctx")),
            P(("dp", "ctx")),
            P(("dp", "ctx")),
            P(("dp", "ctx")),
            P(("dp", "ctx")),
            P(("dp", "ctx")),
            P(("dp", "ctx")),
            P("dp", "ctx", None),
        ),
        out_specs=(
            P("dp", "ctx", None),
            P("dp", "ctx", None),
            P(),
            P(),
            P(("dp", "ctx")),
            P(("dp", "ctx")),
            P(("dp", "ctx")),
            P(("dp", "ctx")),
            P(("dp", "ctx")),
            P(("dp", "ctx")),
            P(("dp", "ctx")),
        ),
        check_vma=False,
    )
```

time: 772 us -> 236 us (0.31); the launches traced: 757 us -> 234 us
  blocking collectives: 381 us -> 0 us
  waiting for transfers between devices: 258 us -> 0 us
  Pallas kernels: 0 us -> 155 us
  local copies, waits for them, and re-layouts: 52.1 us -> 23.3 us
  between operations: 14.7 us -> 1.54 us
    all_gather x6 -> x0, blocking collectives: 339 us -> none  [the longest x1 79.1 us: on_device(): lax.all_gather(w_query, ('dp', 'ctx'), axis=0, tiled=True)]
    unnamed x6 -> x0, waiting for transfers between devices: 212 us -> none
    pallas_call x0 -> x8, Pallas kernels: none -> 155 us  [exchange(): pl.pallas_call(kernel, out_shape=[jax.ShapeDtypeStruct((counts[axis],) +...]
    reduce_scatter x1 -> x0, waiting for transfers between devices: 45.3 us -> none  [on_device(): lax.psum_scatter(key_terms, 'ctx', scatter_dimension=0, tiled=True)]
    psum x1 -> x0, blocking collectives: 41.5 us -> none  [on_device(): gain_sums = lax.psum((gain_term, grad_gffn), ('dp', 'ctx'))]
    reshape x14, local copies, waits for them, and re-layouts: 31.4 us -> 7.02 us  [the longest x5 2.69 us: unpack(): out.append(rows_of[:, start:start + step].reshape(-1, width))]
    all_gather x4 -> x0, other arithmetic: 12.7 us -> none  [the longest x1 5.16 us: on_device(): lax.all_gather(w_out, ('dp', 'ctx'), axis=0, tiled=True)]
    unnamed x101 -> x67, local copies, waits for them, and re-layouts: 16.7 us -> 4.78 us
  transfers between devices with their start and end apart: 5 -> 0, of which waited for: 2 -> 0; matrix products, arithmetic and copies ran while one was open for 9% -> 0% of each run, Pallas kernels for 0% -> 0%
where the time goes in v1:
time: 236 us; the launch traced here: 234 us
  Pallas kernels  155 us (66%)
  other arithmetic  27.5 us (12%)
  matrix products  26.4 us (11%)
  local copies, waits for them, and re-layouts  23.3 us (10%)
    pallas_call x8, Pallas kernels, exchange(): pl.pallas_call(kernel, out_shape=[jax.ShapeDtypeStruct((counts[axis],) +...  155 us
    dot_general x12, matrix products, matmul(): return jnp.dot(left, right, preferred_element_type=jnp.float32)  15.4 us
    reduce_sum x10, other arithmetic, total_of(): return jnp.sum(pieces.astype(jnp.float32), axis=0)  11.6 us
    unnamed x67, local copies, waits for them, and re-layouts  4.78 us

profile of v1, /device:TPU:0, one launch (start us, length us, event | category | flops | bytes accessed | tf_op | source)
XLA Modules:
  0.0 234.0 jit_solution(6043509410354035343)
XLA Ops:
  0.7 0.8 broadcast_multiply_fusion
  1.4 1.4 pad_maximum_fusion.15.refs_0_
  2.9 1.5 pad_maximum_fusion.13.refs_2_
  4.4 1.1 copy.104
  5.7 1.2 copy.105
  6.8 0.7 bitcast_convert_fusion.refs_2_
  7.5 15.0 %shard_map.203 = (bf16[8,216,128]{2,1,0:T(8,128)(2,1)}, s32[8,1,128]{2,1,0:T(1,128)}, bf16[4,128,576]{2,1,0:T(8,128)(2,1)}) custom-call(bf16[216,128]{1,0:T(8,128)(2,1)} %pad_maximum_fusion.15.refs_0_, s32[1,128]{1,0:T(1,128)} %refs_1_.1, bf16[128,576]{1,0:T(8,128)(2,1)} %bitcast_convert_fusion.refs_2_), custom_call_target="tpu_custom_call" | custom-call | tf_op jit(solution)/shard_map/pallas_call | solution.py:107
  22.5 0.9 fusion.29
  23.4 1.0 fusion.54
  24.4 1.1 fusion.53
  25.5 0.9 reshape.359.refs_1_
  26.7 0.8 pad_maximum_fusion.6.refs_0_
  27.6 25.7 %shard_map.204 = (bf16[4,144,960]{2,1,0:T(8,128)(2,1)}, bf16[4,144,576]{2,1,0:T(8,128)(2,1)}, bf16[8,432,128]{2,1,0:T(8,128)(2,1)}) custom-call(bf16[144,960]{1,0:T(8,128)(2,1)} %pad_maximum_fusion.6.refs_0_, bf16[144,576]{1,0:T(8,128)(2,1)} %reshape.359.refs_1_, bf16[432,128]{1,0:T(8,128)(2,1)} %pad_maximum_fusion.13.refs_2_), custom_call_target="tpu_custom_call" | custom-call | tf_op jit(solution)/shard_map/pallas_call | solution.py:107
  53.3 2.1 fusion.36
  55.8 0.7 pad_maximum_fusion.14.refs_0_
  57.2 1.0 maximum_bitcast_fusion.refs_1_
  58.2 17.6 %shard_map.205 = (bf16[8,128,384]{2,1,0:T(8,128)(2,1)}, bf16[4,144,768]{2,1,0:T(8,128)(2,1)}) custom-call(bf16[128,384]{1,0:T(8,128)(2,1)} %pad_maximum_fusion.14.refs_0_, bf16[4,144,768]{2,1,0:T(8,128)(2,1)} %maximum_bitcast_fusion.refs_1_), custom_call_target="tpu_custom_call" | custom-call | tf_op jit(solution)/shard_map/pallas_call | solution.py:107
  75.8 1.5 fusion.52
  77.7 0.9 fusion.5
  78.6 1.0 fusion.2
  79.6 1.2 log_add_fusion
  80.7 1.2 fusion.26
  82.5 0.8 multiply_convert_fusion.4.refs_0_
  83.3 16.9 %shard_map.206 = (bf16[4,128,576]{2,1,0:T(8,128)(2,1)}, bf16[8,216,128]{2,1,0:T(8,128)(2,1)}) custom-call(bf16[128,576]{1,0:T(8,128)(2,1)} %multiply_convert_fusion.4.refs_0_, bf16[216,128]{1,0:T(8,128)(2,1)} %bitcast.212), custom_call_target="tpu_custom_call" | custom-call | tf_op jit(solution)/shard_map/pallas_call | solution.py:107
  100.2 1.4 reshape.372
  101.6 2.2 fusion.56
  103.8 2.0 multiply_convert_fusion.2
  105.8 1.3 convolution_convert_fusion.5
  107.2 1.4 convolution_convert_fusion.3
  108.6 1.7 convolution_convert_fusion.1
  110.3 1.3 copy.117
  111.5 1.5 reshape.376.refs_1_
  113.0 2.2 copy.116
  115.2 14.6 %shard_map.207 = (bf16[4,128,576]{2,1,0:T(8,128)(2,1)}, bf16[8,216,128]{2,1,0:T(8,128)(2,1)}) custom-call(bf16[4,128,576]{2,1,0:T(8,128)(2,1)} %bitcast.180, bf16[8,216,128]{2,1,0:T(8,128)(2,1)} %reshape.376.refs_1_), custom_call_target="tpu_custom_call" | custom-call | tf_op jit(solution)/shard_map/pallas_call | solution.py:107
  129.8 1.3 convert_reduce_fusion.3
  131.3 0.8 bitcast_add_fusion
  133.1 1.1 copy.122
  134.2 1.7 convert_reduce_fusion.4
  135.9 3.6 %fusion.17 = bf16[3,64,1024]{2,1,0:T(8,128)(2,1)S(1)} fusion(bf16[128,3,3,64]{0,3,2,1:T(8,128)(2,1)S(1)} %bitcast.202, f32[3,1024,128,3]{2,1,3,0:T(8,128)} %copy-done, f32[3,3,128]{2,1,0:T(4,128)S(1)} %copy-done.27, pred[128,1024]{0,1:T(8,128)(4,1)S(1)} %fusion.29), kind=kOutput, calls=%fused_computation.28 | convolution fusion | flops 155910144 | bytes 5394944 | tf_op jit(solution)/shard_map/kgqs,qkgd->skd/dot_general | solution.py:330
  139.6 3.8 %fusion.1 = bf16[3,3,128,1024]{2,3,1,0:T(8,128)(2,1)S(1)} fusion(f32[3,1024,128,3]{2,1,3,0:T(8,128)} %copy-done, f32[3,3,128]{2,1,0:T(4,128)S(1)} %bitcast.218, f32[3,3,128]{2,1,0:T(4,128)S(1)} %copy-done.27, pred[128,1024]{0,1:T(8,128)(4,1)S(1)} %fusion.29, bf16[1024,3,64,1]{0,2,3,1:T(8,128)(2,1)S(1)} %bitcast.205, bf16[128,3,3,64]{0,3,2,1:T(8,128)(2,1)S(1)} %bitcast.203), kind=kOutput, calls=%fused_computation.2 | convolution fusion | flops 158072832 | bytes 7758848 | tf_op jit(solution)/shard_map/qkgd,skd->kgqs/dot_general | solution.py:315
  144.4 0.9 fusion.16
  145.9 1.2 pad_maximum_fusion.2.refs_0_
  147.1 1.2 convolution_convert_fusion.2
  148.3 27.7 %shard_map.208 = (bf16[8,128,384]{2,1,0:T(8,128)(2,1)}, bf16[4,128,576]{2,1,0:T(8,128)(2,1)}, bf16[4,144,768]{2,1,0:T(8,128)(2,1)}, bf16[4,144,576]{2,1,0:T(8,128)(2,1)}) custom-call(bf16[8,128,384]{2,1,0:T(8,128)(2,1)} %pad_maximum_fusion.2.refs_0_, bf16[4,128,576]{2,1,0:T(8,128)(2,1)} %bitcast.181, bf16[4,144,768]{2,1,0:T(8,128)(2,1)} %bitcast.194, ...), custom_call_target="tpu_custom_call" | custom-call | tf_op jit(solution)/shard_map/pallas_call | solution.py:107
  176.0 1.2 convert_reduce_fusion.2
  177.4 0.9 copy.130
  178.2 1.2 reduce_sum.181
  179.7 1.3 convert_reduce_fusion.1
  181.5 0.6 multiply_reduce_fusion.1
  182.1 0.6 pad_maximum_fusion.17.refs_0_
  182.9 0.9 copy.131
  183.7 1.6 convolution_convert_fusion
  186.1 1.0 pad_maximum_fusion.refs_2_
  187.1 20.3 %shard_map.209 = (f32[4,2,576]{2,1,0:T(2,128)}, bf16[4,144,960]{2,1,0:T(8,128)(2,1)}, bf16[8,432,128]{2,1,0:T(8,128)(2,1)}) custom-call(f32[2,576]{1,0:T(2,128)} %pad_maximum_fusion.17.refs_0_, bf16[4,144,960]{2,1,0:T(8,128)(2,1)} %bitcast.172, bf16[8,432,128]{2,1,0:T(8,128)(2,1)} %pad_maximum_fusion.refs_2_), custom_call_target="tpu_custom_call" | custom-call | tf_op jit(solution)/shard_map/pallas_call | solution.py:107
  207.4 1.4 reduce_sum.179.refs_0_
  208.8 1.3 convert_reduce_fusion
  210.1 0.7 slice_bitcast_fusion.2
  211.7 0.9 pad_maximum_fusion.5.refs_1_
  212.6 17.7 %shard_map.210 = (f32[8,2,576]{2,1,0:T(2,128)}, bf16[8,216,128]{2,1,0:T(8,128)(2,1)}) custom-call(f32[2,576]{1,0:T(2,128)} %reduce_sum.179.refs_0_, bf16[8,216,128]{2,1,0:T(8,128)(2,1)} %pad_maximum_fusion.5.refs_1_), custom_call_target="tpu_custom_call" | custom-call | tf_op jit(solution)/shard_map/pallas_call | solution.py:107
  230.3 0.8 reduce_sum.182
  231.1 0.6 slice_reduce_fusion
  231.7 1.1 convert_reduce_fusion.5
  232.8 0.6 slice_bitcast_fusion.6
  233.4 0.6 slice_bitcast_fusion.4
  (116 shorter events, 7.7 us)
Async XLA Ops:
  0.6 21.8 %copy-start.29 = (s32[1,128]{1,0:T(1,128)S(1)}, s32[1,128]{1,0:T(1,128)}, u32[]{:S(2)}) copy-start(s32[1,128]{1,0:T(1,128)} %refs_1_.1) | copy-start | bytes 1540
  1.4 54.0 %copy-start.18 = (f32[128,32]{0,1:T(8,128)}, f32[128,32]{0,1:T(8,128)S(1)}, u32[]{:S(2)}) copy-start(f32[128,32]{0,1:T(8,128)S(1)} %get-tuple-element.130) | copy-start | bytes 49156
  5.6 47.7 %copy-start.10 = (f32[1,128,576]{1,2,0:T(8,128)S(1)}, f32[1,128,576]{1,2,0:T(8,128)}, u32[]{:S(2)}) copy-start(f32[1,128,576]{1,2,0:T(8,128)} %param.12) | copy-start | bytes 884740
  5.6 47.7 %copy-start.21 = (f32[576]{0:T(1024)S(1)}, f32[576]{0:T(1024)}, u32[]{:S(2)}) copy-start(f32[576]{0:T(1024)} %param.14) | copy-start | bytes 6916
  5.6 49.8 %copy-start.25 = (f32[128]{0:T(128)}, f32[128]{0:T(128)S(1)}, u32[]{:S(2)}) copy-start(f32[128]{0:T(128)S(1)} %add_rsqrt_fusion.1) | copy-start | bytes 1540
  53.3 3.3 %copy-start.13 = (bf16[8,432,128]{2,1,0:T(8,128)(2,1)S(1)}, bf16[8,432,128]{2,1,0:T(8,128)(2,1)}, u32[]{:S(2)}) copy-start(bf16[8,432,128]{2,1,0:T(8,128)(2,1)} %get-tuple-element.35) | copy-start | bytes 2654212
  55.7 22.0 %copy-start.3 = (bf16[128,9,64]{0,2,1:T(8,128)(2,1)}, bf16[128,9,64]{0,2,1:T(8,128)(2,1)S(1)}, u32[]{:S(2)}) copy-start(bf16[128,9,64]{0,2,1:T(8,128)(2,1)S(1)} %pad_maximum_fusion.12) | copy-start | bytes 442372
  77.7 3.1 %copy-start.16 = (bf16[1024,192]{0,1:T(8,128)(2,1)}, bf16[1024,192]{0,1:T(8,128)(2,1)S(1)}, u32[]{:S(2)}) copy-start(bf16[1024,192]{0,1:T(8,128)(2,1)S(1)} %copy.111) | copy-start | bytes 1179652
  78.6 2.2 copy-start
  80.7 1.3 copy-start.2
  80.7 1.7 copy-start.23
  82.0 21.8 %copy-start.7 = (bf16[128,3,3,64]{0,3,2,1:T(8,128)(2,1)}, bf16[128,3,3,64]{0,3,2,1:T(8,128)(2,1)S(1)}, u32[]{:S(2)}) copy-start(bf16[128,3,3,64]{0,3,2,1:T(8,128)(2,1)S(1)} %fusion.26) | copy-start | bytes 442372
  82.5 48.6 %copy-start.28 = (f32[128]{0:T(128)}, f32[128]{0:T(128)S(1)}, u32[]{:S(2)}) copy-start(f32[128]{0:T(128)S(1)} %add_rsqrt_fusion) | copy-start | bytes 1540
  103.8 2.0 copy-start.14
  103.8 3.3 %copy-start.12 = (bf16[4,144,768]{2,1,0:T(8,128)(2,1)S(1)}, bf16[4,144,768]{2,1,0:T(8,128)(2,1)}, u32[]{:S(2)}) copy-start(bf16[4,144,768]{2,1,0:T(8,128)(2,1)} %get-tuple-element.41) | copy-start | bytes 2654212
  105.8 2.8 %copy-start.5 = (bf16[512,384]{0,1:T(8,128)(2,1)}, bf16[512,384]{0,1:T(8,128)(2,1)S(1)}, u32[]{:S(2)}) copy-start(bf16[512,384]{0,1:T(8,128)(2,1)S(1)} %get-tuple-element.105) | copy-start | bytes 1179652
  105.8 2.8 %copy-start.15 = (bf16[4,128,576]{2,1,0:T(8,128)(2,1)S(1)}, bf16[4,128,576]{2,1,0:T(8,128)(2,1)}, u32[]{:S(2)}) copy-start(bf16[4,128,576]{2,1,0:T(8,128)(2,1)} %get-tuple-element.40) | copy-start | bytes 1769476
  113.0 18.3 %copy-start.24 = (f32[576]{0:T(1024)S(1)}, f32[576]{0:T(1024)}, u32[]{:S(2)}) copy-start(f32[576]{0:T(1024)} %param.15) | copy-start | bytes 6916
  129.8 2.7 %copy-start.8 = (bf16[128,3,3,64]{0,3,2,1:T(8,128)(2,1)S(1)}, bf16[128,3,3,64]{0,3,2,1:T(8,128)(2,1)}, u32[]{:S(2)}) copy-start(bf16[128,3,3,64]{0,3,2,1:T(8,128)(2,1)} %copy-done.7) | copy-start | bytes 442372
  129.8 2.8 %copy-start.6 = (bf16[512,384]{0,1:T(8,128)(2,1)S(1)}, bf16[512,384]{0,1:T(8,128)(2,1)}, u32[]{:S(2)}) copy-start(bf16[512,384]{0,1:T(8,128)(2,1)} %copy-done.5) | copy-start | bytes 1179652
  132.1 3.8 %copy-start.27 = (f32[3,3,128]{2,1,0:T(4,128)S(1)}, f32[3,3,128]{2,1,0:T(4,128)}, u32[]{:S(2)}) copy-start(f32[3,3,128]{2,1,0:T(4,128)} %log_add_fusion) | copy-start | bytes 13828
  135.9 3.6 %copy-start.17 = (bf16[1024,192]{0,1:T(8,128)(2,1)S(1)}, bf16[1024,192]{0,1:T(8,128)(2,1)}, u32[]{:S(2)}) copy-start(bf16[1024,192]{0,1:T(8,128)(2,1)} %copy-done.16) | copy-start | bytes 1179652
  143.4 0.9 copy-start.4
  177.3 4.1 %copy-start.19 = (f32[128,32]{0,1:T(8,128)S(1)}, f32[128,32]{0,1:T(8,128)}, u32[]{:S(2)}) copy-start(f32[128,32]{0,1:T(8,128)} %copy-done.18) | copy-start | bytes 49156
  177.3 4.1 %copy-start.20 = (f32[128,32]{0,1:T(8,128)S(1)}, f32[128,32]{0,1:T(8,128)}, u32[]{:S(2)}) copy-start(f32[128,32]{0,1:T(8,128)} %get-tuple-element.128) | copy-start | bytes 49156
  177.3 4.1 %copy-start.1 = (bf16[4,144,960]{2,1,0:T(8,128)(2,1)S(1)}, bf16[4,144,960]{2,1,0:T(8,128)(2,1)}, u32[]{:S(2)}) copy-start(bf16[4,144,960]{2,1,0:T(8,128)(2,1)} %get-tuple-element.34) | copy-start | bytes 3317764
  177.3 4.1 %copy-start.22 = (f32[576]{0:T(1024)S(1)}, f32[576]{0:T(1024)}, u32[]{:S(2)}) copy-start(f32[576]{0:T(1024)} %param.14) | copy-start | bytes 6916
  177.4 4.1 %copy-start.26 = (f32[128]{0:T(128)S(1)}, f32[128]{0:T(128)}, u32[]{:S(2)}) copy-start(f32[128]{0:T(128)} %copy-done.25) | copy-start | bytes 1540
  182.1 3.2 %copy-start.11 = (bf16[4,144,768]{2,1,0:T(8,128)(2,1)S(1)}, bf16[4,144,768]{2,1,0:T(8,128)(2,1)}, u32[]{:S(2)}) copy-start(bf16[4,144,768]{2,1,0:T(8,128)(2,1)} %get-tuple-element.45) | copy-start | bytes 2654212
  207.4 3.5 %copy-start.9 = (bf16[4,144,960]{2,1,0:T(8,128)(2,1)S(1)}, bf16[4,144,960]{2,1,0:T(8,128)(2,1)}, u32[]{:S(2)}) copy-start(bf16[4,144,960]{2,1,0:T(8,128)(2,1)} %get-tuple-element.47) | copy-start | bytes 3317764

commit v2 on v1

--- a/solution.py
+++ b/solution.py
@@ -53,72 +53,162 @@
 
 
 def exchange(collective_id, *items):
-    arrays = [array for array, _, _ in items]
+    arrays = []
+    counts = {axis: lax.axis_size(axis) for _, axis, _ in items}
+    axes = sorted(counts)
+    shapes = []
+    staging = []
+    slot_of = {}
+    for index, (array, axis, mode) in enumerate(items):
+        count = counts[axis]
+        shape = array.shape
+        if mode == "gather":
+            shape = (count,) + shape
+        elif mode == "sum":
+            array = array.reshape((count // 2, 2) + shape[1:])
+            shape = (count // 2,) + shape[1:]
+            slot_of[index] = len(staging)
+            staging += [pltpu.VMEM(shape, array.dtype), pltpu.VMEM(shape, array.dtype)]
+        arrays.append(array)
+        shapes.append(jax.ShapeDtypeStruct(shape, array.dtype))
     total = len(items)
-    axes = sorted({axis for _, axis, _ in items})
-    counts = {axis: lax.axis_size(axis) for axis in axes}
     most = max(counts.values())
 
     def kernel(*refs):
         sources, targets = refs[:total], refs[total : 2 * total]
-        send_sem, recv_sem, own_sem = refs[2 * total :]
+        send_sem, recv_sem, own_sem = refs[2 * total : 2 * total + 3]
+        stages = refs[2 * total + 3 :]
         place = {axis: lax.axis_index(axis) for axis in axes}
 
-        def piece(index, peer):
-            return sources[index] if items[index][2] else sources[index].at[peer]
-
-        def partner(axis, step):
-            return lax.rem(place[axis] + step, counts[axis])
+        def ahead(axis, step):
+            return lax.rem(place[axis] + step + counts[axis], counts[axis])
+
+        def sibling(axis):
+            return place[axis] + 1 - 2 * lax.rem(place[axis], 2)
+
+        def remote(source, target, index, slot, peer):
+            copy = pltpu.make_async_remote_copy(
+                src_ref=source,
+                dst_ref=target,
+                send_sem=send_sem.at[index, slot],
+                recv_sem=recv_sem.at[index, slot],
+                device_id={items[index][1]: peer},
+                device_id_type=pl.DeviceIdType.MESH,
+            )
+            copy.start()
+            return copy
 
         barrier = pltpu.get_barrier_semaphore()
+        greeted = 0
         for axis in axes:
-            for step in range(1, counts[axis]):
+            whole = any(mode == "swap" and axis == other for _, other, mode in items)
+            steps = range(1, counts[axis]) if whole else range(2, counts[axis], 2)
+            peers = [ahead(axis, step) for step in steps]
+            if not whole:
+                peers.append(sibling(axis))
+            for peer in peers:
                 pl.semaphore_signal(
-                    barrier,
-                    inc=1,
-                    device_id={axis: partner(axis, step)},
-                    device_id_type=pl.DeviceIdType.MESH,
+                    barrier, inc=1, device_id={axis: peer}, device_id_type=pl.DeviceIdType.MESH
                 )
-        started = []
-        for index, (_, axis, _) in enumerate(items):
+            greeted += len(peers)
+        open_copies = []
+        loads = {}
+        for index, (_, axis, mode) in enumerate(items):
             me = place[axis]
-            copy = pltpu.make_async_copy(piece(index, me), targets[index].at[me], own_sem.at[index])
+            if mode == "sum":
+                copy = pltpu.make_async_copy(
+                    sources[index].at[:, lax.rem(me, 2)],
+                    stages[slot_of[index]],
+                    own_sem.at[index, 0],
+                )
+                loads[index] = [copy]
+            else:
+                own = sources[index] if mode == "gather" else sources[index].at[me]
+                copy = pltpu.make_async_copy(own, targets[index].at[me], own_sem.at[index, 0])
+                open_copies.append(copy)
             copy.start()
-            started.append(copy)
-        pl.semaphore_wait(barrier, sum(counts[axis] - 1 for axis in axes))
-        for step in range(1, most):
-            for index, (_, axis, _) in enumerate(items):
-                if step >= counts[axis]:
-                    continue
-                peer = partner(axis, step)
-                copy = pltpu.make_async_remote_copy(
-                    src_ref=piece(index, peer),
-                    dst_ref=targets[index].at[place[axis]],
-                    send_sem=send_sem.at[index, step],
-                    recv_sem=recv_sem.at[index, step],
-                    device_id={axis: peer},
-                    device_id_type=pl.DeviceIdType.MESH,
+        pl.semaphore_wait(barrier, greeted)
+        arriving = {}
+        for index, (_, axis, mode) in enumerate(items):
+            me = place[axis]
+            if mode == "sum":
+                loads[index].append(
+                    remote(
+                        sources[index].at[:, 1 - lax.rem(me, 2)],
+                        stages[slot_of[index] + 1],
+                        index,
+                        0,
+                        sibling(axis),
+                    )
                 )
-                copy.start()
-                started.append(copy)
-        for copy in started:
+            elif mode == "gather":
+                for step in range(2, counts[axis], 2):
+                    arriving[index, step] = remote(
+                        sources[index], targets[index].at[me], index, step, ahead(axis, step)
+                    )
+                open_copies.append(
+                    remote(sources[index], targets[index].at[me], index, 1, sibling(axis))
+                )
+        for index, (_, axis, mode) in enumerate(items):
+            if mode == "swap":
+                for step in range(1, counts[axis]):
+                    peer = ahead(axis, step)
+                    open_copies.append(
+                        remote(
+                            sources[index].at[peer],
+                            targets[index].at[place[axis]],
+                            index,
+                            step,
+                            peer,
+                        )
+                    )
+        for index, (_, axis, mode) in enumerate(items):
+            if mode != "sum":
+                continue
+            mine, other = stages[slot_of[index]], stages[slot_of[index] + 1]
+            for copy in loads[index]:
+                copy.wait()
+
+            def add(row, carry):
+                mine[row] = (
+                    mine[row].astype(jnp.float32) + other[row].astype(jnp.float32)
+                ).astype(mine.dtype)
+                return carry
+
+            lax.fori_loop(0, counts[axis] // 2, add, 0)
+            here = place[axis] // 2
+            for step in range(2, counts[axis], 2):
+                peer = ahead(axis, step)
+                open_copies.append(
+                    remote(mine.at[peer // 2], targets[index].at[here], index, step, peer)
+                )
+            copy = pltpu.make_async_copy(
+                mine.at[here], targets[index].at[here], own_sem.at[index, 1]
+            )
+            copy.start()
+            open_copies.append(copy)
+        for step in range(2, most, 2):
+            for index, (_, axis, mode) in enumerate(items):
+                if mode == "gather" and step < counts[axis]:
+                    arriving[index, step].wait_recv()
+                    block = targets[index].at[ahead(axis, -step)]
+                    open_copies.append(remote(block, block, index, step + 1, sibling(axis)))
+        for copy in arriving.values():
+            copy.wait_send()
+        for copy in open_copies:
             copy.wait()
 
     return pl.pallas_call(
         kernel,
-        out_shape=[
-            jax.ShapeDtypeStruct(
-                (counts[axis],) + array.shape if whole else array.shape, array.dtype
-            )
-            for array, axis, whole in items
-        ],
+        out_shape=shapes,
         in_specs=[pl.BlockSpec(memory_space=pl.ANY)] * total,
         out_specs=[pl.BlockSpec(memory_space=pl.ANY)] * total,
         scratch_shapes=[
             pltpu.SemaphoreType.DMA((total, most)),
             pltpu.SemaphoreType.DMA((total, most)),
-            pltpu.SemaphoreType.DMA((total,)),
-        ],
+            pltpu.SemaphoreType.DMA((total, 2)),
+        ]
+        + staging,
         compiler_params=pltpu.CompilerParams(collective_id=collective_id, has_side_effects=True),
     )(*arrays)
 
@@ -202,16 +292,16 @@
     attn_flat = (w_query, w_key, w_value, w_out)
     attn_lengths = [w.shape[0] for w in attn_flat]
     got_attn, got_segs, all_cot = exchange(
-        1, (pack(attn_flat), "ctx", True), (segment_ids, "ctx", True), (cot_low, "dp", True)
+        1, (pack(attn_flat), "ctx", "gather"), (segment_ids, "ctx", "gather"), (cot_low, "dp", "gather")
     )
     all_cot = all_cot.reshape(-1, D)
     all_segs = got_segs.reshape(seq_rows)
     slabs = unpack(got_attn, attn_lengths, (H * HD, KV * HD, KV * HD, D))
     mat_qkv, mat_out, got_gate_up = exchange(
         2,
-        (jnp.concatenate(slabs[:3], axis=1), "dp", True),
-        (slabs[3], "dp", True),
-        (pack((w_gate, w_up)), "ctx", True),
+        (jnp.concatenate(slabs[:3], axis=1), "dp", "gather"),
+        (slabs[3], "dp", "gather"),
+        (pack((w_gate, w_up)), "ctx", "gather"),
     )
     mat_qkv = mat_qkv.reshape(D, -1)
     mat_out = mat_out.reshape(H * HD, D)
@@ -235,7 +325,7 @@
     packed_kv = jnp.concatenate(
         [turned[:, H:].reshape(span_rows, KV * HD), qkv[:, (H + KV) * HD :].astype(low)], axis=1
     )
-    all_kv, mat_gu = exchange(3, (packed_kv, "ctx", True), (gate_up, "dp", False))
+    all_kv, mat_gu = exchange(3, (packed_kv, "ctx", "gather"), (gate_up, "dp", "swap"))
     mat_gu = mat_gu.reshape(D, 2 * ff_part)
     all_kv = all_kv.reshape(seq_rows, 2 * KV * HD)
     all_keys = all_kv[:, : KV * HD].reshape(seq_rows, KV, HD)
@@ -272,7 +362,7 @@
     normed_ffn = (hidden * inv_ffn * gain_ffn).astype(low)
 
     all_normed, got_down = exchange(
-        4, (normed_ffn, "dp", True), (pack((w_down,)), "ctx", True)
+        4, (normed_ffn, "dp", "gather"), (pack((w_down,)), "ctx", "gather")
     )
     (mat_down,) = unpack(got_down, (w_down.shape[0],), (D,))
     all_normed = all_normed.reshape(-1, D)
@@ -290,7 +380,7 @@
     grad_down = matmul(mixed.T, all_cot).astype(low)
     grad_gu = matmul(all_normed.T, grad_gu_act).astype(low).reshape(dp_count, d_part, -1)
     got_normed, got_down_grad = exchange(
-        5, (part_normed, "dp", False), (pack_grads((grad_down,), ctx_count), "ctx", False)
+        5, (part_normed, "dp", "sum"), (pack_grads((grad_down,), ctx_count), "ctx", "sum")
     )
     grad_normed_ffn = total_of(got_normed)
 
@@ -340,17 +430,9 @@
             ).astype(low)
         )
     key_terms = jnp.concatenate(key_terms, axis=0).reshape(ctx_count, span_rows, 2 * KV * HD)
-    got_terms, got_out, got_gu, got_out_grad = exchange(
-        6,
-        (key_terms, "ctx", False),
-        (part_out, "dp", False),
-        (grad_gu, "dp", False),
-        (grad_out.astype(low).reshape(dp_count, H * HD // dp_count, D), "dp", False),
-    )
-    out_rows = hidden + total_of(got_out)
+    got_terms, got_gu = exchange(6, (key_terms, "ctx", "sum"), (grad_gu, "dp", "swap"))
     slab_gate = got_gu[:, :, :ff_part].transpose(1, 0, 2).reshape(d_part, FF)
     slab_up = got_gu[:, :, ff_part:].transpose(1, 0, 2).reshape(d_part, FF)
-    slab_out = total_of(got_out_grad).astype(low)
     own_grads = total_of(got_terms)
     grad_qk = rotate(
         jnp.concatenate(
@@ -374,25 +456,29 @@
     grad_rows = grad_hidden + grad_res_attn
 
     gain_terms = jnp.stack([grad_gattn, grad_gffn])
-    got_gains, got_qkv, got_gu_grad = exchange(
+    got_gains, got_qkv, got_out_grad, got_gu_grad = exchange(
         7,
-        (gain_terms, "dp", True),
-        (grad_mat_qkv.astype(low).reshape(dp_count, d_part, -1), "dp", False),
-        (pack_grads((slab_gate, slab_up), ctx_count), "ctx", False),
+        (gain_terms, "dp", "gather"),
+        (grad_mat_qkv.astype(low).reshape(dp_count, d_part, -1), "dp", "sum"),
+        (grad_out.astype(low).reshape(dp_count, H * HD // dp_count, D), "dp", "sum"),
+        (pack_grads((slab_gate, slab_up), ctx_count), "ctx", "sum"),
     )
     slab_qkv = total_of(got_qkv).astype(low)
+    slab_out = total_of(got_out_grad).astype(low)
     attn_slabs = (
         slab_qkv[:, : H * HD],
         slab_qkv[:, H * HD : (H + KV) * HD],
         slab_qkv[:, (H + KV) * HD :],
         slab_out,
     )
-    got_gains, got_attn_grad = exchange(
+    got_gains, got_out, got_attn_grad = exchange(
         8,
-        (total_of(got_gains), "ctx", True),
-        (pack_grads(attn_slabs, ctx_count), "ctx", False),
+        (total_of(got_gains), "ctx", "gather"),
+        (part_out, "dp", "sum"),
+        (pack_grads(attn_slabs, ctx_count), "ctx", "sum"),
     )
     gains = total_of(got_gains)
+    out_rows = hidden + total_of(got_out)
     reduced = (
         unpack_grads(total_of(got_attn_grad), attn_lengths)
         + unpack_grads(total_of(got_gu_grad), (w_gate.shape[0], w_up.shape[0]))

time: 236 us -> 215 us (0.911)
  Pallas kernels: 155 us -> 136 us
  other arithmetic: 27.5 us -> 22.9 us
  local copies, waits for them, and re-layouts: 23.3 us -> 26.2 us
    pallas_call x8, Pallas kernels: 155 us -> 136 us  [exchange(): pl.pallas_call(kernel, out_shape=shapes, in_specs=[pl.BlockSpec(memory_sp...]
    unnamed x67 -> x53, local copies, waits for them, and re-layouts: 4.78 us -> 5.72 us
where the time goes in v2:
time: 215 us; the launch traced here: 214 us
  Pallas kernels  136 us (63%)
  matrix products  27.1 us (13%)
  local copies, waits for them, and re-layouts  26.2 us (12%)
  other arithmetic  22.9 us (11%)
    pallas_call x8, Pallas kernels, exchange(): pl.pallas_call(kernel, out_shape=shapes, in_specs=[pl.BlockSpec(memory_sp...  136 us
    dot_general x12, matrix products, matmul(): return jnp.dot(left, right, preferred_element_type=jnp.float32)  15.4 us
    reduce_sum x10, other arithmetic, total_of(): return jnp.sum(pieces.astype(jnp.float32), axis=0)  9.33 us
    unnamed x53, local copies, waits for them, and re-layouts  5.72 us
    dot_general x1, matrix products, on_device(): jnp.einsum('kgqs,qkgd->skd', probs.astype(low), grad_grouped, preferred_e...  4.38 us

profile of v2, /device:TPU:0, one launch (start us, length us, event | category | flops | bytes accessed | tf_op | source)
XLA Modules:
  0.0 214.0 jit_solution(9130519720076598309)
XLA Ops:
  0.8 1.4 pad_maximum_fusion.15.refs_0_
  2.3 1.5 pad_maximum_fusion.13.refs_2_
  3.8 1.1 copy.104
  5.0 1.2 copy.105
  6.2 0.7 bitcast_convert_fusion.refs_2_
  6.9 15.9 %shard_map.203 = (bf16[8,216,128]{2,1,0:T(8,128)(2,1)}, s32[8,1,128]{2,1,0:T(1,128)}, bf16[4,128,576]{2,1,0:T(8,128)(2,1)}) custom-call(bf16[216,128]{1,0:T(8,128)(2,1)} %pad_maximum_fusion.15.refs_0_, s32[1,128]{1,0:T(1,128)} %refs_1_.1, bf16[128,576]{1,0:T(8,128)(2,1)} %bitcast_convert_fusion.refs_2_), custom_call_target="tpu_custom_call" | custom-call | tf_op jit(solution)/shard_map/pallas_call | solution.py:201
  22.9 0.9 fusion.33
  23.8 1.0 fusion.58
  24.8 1.1 fusion.57
  25.8 0.9 reshape.349.refs_1_
  27.1 0.8 pad_maximum_fusion.6.refs_0_
  27.9 20.0 %shard_map.204 = (bf16[4,144,960]{2,1,0:T(8,128)(2,1)}, bf16[4,144,576]{2,1,0:T(8,128)(2,1)}, bf16[8,432,128]{2,1,0:T(8,128)(2,1)}) custom-call(bf16[144,960]{1,0:T(8,128)(2,1)} %pad_maximum_fusion.6.refs_0_, bf16[144,576]{1,0:T(8,128)(2,1)} %reshape.349.refs_1_, bf16[432,128]{1,0:T(8,128)(2,1)} %pad_maximum_fusion.13.refs_2_), custom_call_target="tpu_custom_call" | custom-call | tf_op jit(solution)/shard_map/pallas_call | solution.py:201
  48.0 2.1 fusion.40
  50.5 0.7 pad_maximum_fusion.14.refs_0_
  51.9 1.0 maximum_bitcast_fusion.refs_1_
  52.9 17.8 %shard_map.205 = (bf16[8,128,384]{2,1,0:T(8,128)(2,1)}, bf16[4,144,768]{2,1,0:T(8,128)(2,1)}) custom-call(bf16[128,384]{1,0:T(8,128)(2,1)} %pad_maximum_fusion.14.refs_0_, bf16[4,144,768]{2,1,0:T(8,128)(2,1)} %maximum_bitcast_fusion.refs_1_), custom_call_target="tpu_custom_call" | custom-call | tf_op jit(solution)/shard_map/pallas_call | solution.py:201
  70.6 1.5 fusion.56
  72.5 0.9 fusion.5
  73.4 1.0 fusion.2
  74.4 1.1 copy-done
  75.5 1.2 fusion.30
  77.3 0.8 multiply_convert_fusion.4.refs_0_
  78.0 11.4 %shard_map.206 = (bf16[4,128,576]{2,1,0:T(8,128)(2,1)}, bf16[8,216,128]{2,1,0:T(8,128)(2,1)}) custom-call(bf16[128,576]{1,0:T(8,128)(2,1)} %multiply_convert_fusion.4.refs_0_, bf16[216,128]{1,0:T(8,128)(2,1)} %bitcast.210), custom_call_target="tpu_custom_call" | custom-call | tf_op jit(solution)/shard_map/pallas_call | solution.py:201
  89.4 1.4 reshape.362
  90.8 2.2 %fusion.60 = f32[512,768]{0,1:T(8,128)S(1)} fusion(bf16[512,576]{1,0:T(8,128)(2,1)} %bitcast.198, bf16[576,768]{1,0:T(8,128)(2,1)} %bitcast.194), kind=kOutput, calls=%fused_computation.128 | convolution fusion | flops 452984832 | bytes 3047424 | tf_op jit(solution)/shard_map/dot_general | solution.py:20
  93.1 2.0 multiply_convert_fusion.2
  95.1 1.3 convolution_convert_fusion.5
  96.4 1.4 convolution_convert_fusion.3
  97.8 1.7 convolution_convert_fusion.1
  99.5 1.3 copy.117
  100.8 1.5 reshape_reshape.27.refs_1_
  102.3 2.2 %copy.116 = bf16[512,576]{1,0:T(8,128)(2,1)} copy(bf16[512,576]{0,1:T(8,128)(2,1)} %convolution_convert_fusion.3) | data formatting | bytes 1179648 | tf_op jit(solution)/shard_map/convert_element_type | solution.py:379
  104.5 12.8 %shard_map.207 = (bf16[2,128,576]{2,1,0:T(8,128)(2,1)}, bf16[4,216,128]{2,1,0:T(8,128)(2,1)}) custom-call(bf16[2,2,128,576]{3,2,1,0:T(8,128)(2,1)} %bitcast.183, bf16[4,2,216,128]{3,2,1,0:T(8,128)(2,1)} %reshape_reshape.27.refs_1_), custom_call_target="tpu_custom_call" | custom-call | tf_op jit(solution)/shard_map/pallas_call | solution.py:201
  117.2 1.1 convert_reduce_fusion.3
  119.1 0.5 convolution_convert_fusion.4
  119.7 1.1 copy.128
  120.8 1.6 convert_reduce_fusion.4
  122.4 4.4 %fusion.20 = bf16[1024,3,64]{0,2,1:T(8,128)(2,1)} fusion(bf16[128,3,3,64]{0,3,2,1:T(8,128)(2,1)S(1)} %bitcast.201, f32[3,1024,128,3]{2,1,3,0:T(8,128)} %copy-done, f32[3,3,128]{2,1,0:T(4,128)S(1)} %log_add_fusion, pred[128,1024]{0,1:T(8,128)(4,1)S(1)} %copy-done.10), kind=kOutput, calls=%fused_computation.25 | convolution fusion | flops 155910144 | bytes 5394944 | tf_op jit(solution)/shard_map/kgqs,qkgd->skd/dot_general | solution.py:420
  126.8 3.9 %fusion.1 = bf16[3,3,128,1024]{2,3,1,0:T(8,128)(2,1)S(1)} fusion(f32[3,1024,128,3]{2,1,3,0:T(8,128)} %copy-done, f32[3,3,128]{2,1,0:T(4,128)S(1)} %bitcast.216, f32[3,3,128]{2,1,0:T(4,128)S(1)} %log_add_fusion, pred[128,1024]{0,1:T(8,128)(4,1)S(1)} %copy-done.10, bf16[1024,3,64,1]{0,2,3,1:T(8,128)(2,1)S(1)} %bitcast.204, ...), kind=kOutput, calls=%fused_computation.2 | convolution fusion | flops 158072832 | bytes 7758848 | tf_op jit(solution)/shard_map/qkgd,skd->kgqs/dot_general | solution.py:405
  130.6 0.5 convolution_multiply_fusion
  131.5 0.9 fusion.23
  132.7 1.3 concatenate.69
  135.0 1.2 pad_maximum_fusion.2.refs_0_
  136.1 21.4 %shard_map.208 = (bf16[4,128,384]{2,1,0:T(8,128)(2,1)}, bf16[4,144,768]{2,1,0:T(8,128)(2,1)}) custom-call(bf16[4,2,128,384]{3,2,1,0:T(8,128)(2,1)} %pad_maximum_fusion.2.refs_0_, bf16[4,144,768]{2,1,0:T(8,128)(2,1)} %bitcast.193), custom_call_target="tpu_custom_call" | custom-call | tf_op jit(solution)/shard_map/pallas_call | solution.py:201
  157.6 1.1 convert_reduce_fusion.1
  159.1 0.6 multiply_reduce_fusion
  159.9 0.9 copy.131
  160.8 0.6 pad_maximum_fusion.17.refs_0_
  161.4 1.2 convolution_convert_fusion.2
  162.6 1.6 convolution_convert_fusion
  165.0 1.0 pad_maximum_fusion.refs_3_
  166.0 21.9 %shard_map.209 = (f32[4,2,576]{2,1,0:T(2,128)}, bf16[2,144,960]{2,1,0:T(8,128)(2,1)}, bf16[2,144,576]{2,1,0:T(8,128)(2,1)}, bf16[4,432,128]{2,1,0:T(8,128)(2,1)}) custom-call(f32[2,576]{1,0:T(2,128)} %pad_maximum_fusion.17.refs_0_, bf16[2,2,144,960]{3,2,1,0:T(8,128)(2,1)} %bitcast.174, bf16[2,2,144,576]{3,2,1,0:T(8,128)(2,1)} %bitcast.181, ...), custom_call_target="tpu_custom_call" | custom-call | tf_op jit(solution)/shard_map/pallas_call | solution.py:201
  187.9 1.3 reduce_sum.177.refs_0_
  189.2 1.1 reduce_sum.179
  190.3 1.2 reduce_sum.178
  192.4 0.9 pad_maximum_fusion.5.refs_2_
  193.3 15.2 %shard_map.210 = (f32[8,2,576]{2,1,0:T(2,128)}, bf16[2,128,576]{2,1,0:T(8,128)(2,1)}, bf16[4,216,128]{2,1,0:T(8,128)(2,1)}) custom-call(f32[2,576]{1,0:T(2,128)} %reduce_sum.177.refs_0_, bf16[2,2,128,576]{3,2,1,0:T(8,128)(2,1)} %bitcast.182, bf16[4,2,216,128]{3,2,1,0:T(8,128)(2,1)} %pad_maximum_fusion.5.refs_2_), custom_call_target="tpu_custom_call" | custom-call | tf_op jit(solution)/shard_map/pallas_call | solution.py:201
  208.5 1.1 convert_reduce_fusion.2
  209.7 0.9 copy.130
  210.5 0.8 reduce_sum.182
  211.3 0.6 slice_reduce_fusion
  212.0 0.6 slice_bitcast_fusion.6
  212.6 0.6 slice_bitcast_fusion.4
  213.3 0.7 slice_bitcast_fusion.2
  (104 shorter events, 7.3 us)
Async XLA Ops:
  0.6 22.2 %copy-start.23 = (s32[1,128]{1,0:T(1,128)S(1)}, s32[1,128]{1,0:T(1,128)}, u32[]{:S(2)}) copy-start(s32[1,128]{1,0:T(1,128)} %refs_1_.1) | copy-start | bytes 1540
  5.0 43.0 %copy-start.11 = (f32[1,128,576]{1,2,0:T(8,128)S(1)}, f32[1,128,576]{1,2,0:T(8,128)}, u32[]{:S(2)}) copy-start(f32[1,128,576]{1,2,0:T(8,128)} %param.12) | copy-start | bytes 884740
  5.0 43.0 %copy-start.21 = (f32[576]{0:T(1024)S(1)}, f32[576]{0:T(1024)}, u32[]{:S(2)}) copy-start(f32[576]{0:T(1024)} %param.14) | copy-start | bytes 6916
  23.7 50.7 %copy-start.9 = (pred[128,1024]{0,1:T(8,128)(4,1)}, pred[128,1024]{0,1:T(8,128)(4,1)S(1)}, u32[]{:S(2)}) copy-start(pred[128,1024]{0,1:T(8,128)(4,1)S(1)} %fusion.33) | copy-start | bytes 393220
  48.0 3.2 %copy-start.14 = (bf16[8,432,128]{2,1,0:T(8,128)(2,1)S(1)}, bf16[8,432,128]{2,1,0:T(8,128)(2,1)}, u32[]{:S(2)}) copy-start(bf16[8,432,128]{2,1,0:T(8,128)(2,1)} %get-tuple-element.35) | copy-start | bytes 2654212
  50.3 22.2 %copy-start.3 = (bf16[128,9,64]{0,2,1:T(8,128)(2,1)}, bf16[128,9,64]{0,2,1:T(8,128)(2,1)S(1)}, u32[]{:S(2)}) copy-start(bf16[128,9,64]{0,2,1:T(8,128)(2,1)S(1)} %pad_maximum_fusion.12) | copy-start | bytes 442372
  72.5 1.9 copy-start.18
  73.4 2.1 copy-start
  75.5 1.3 copy-start.2
  75.5 1.7 copy-start.22
  76.8 16.2 %copy-start.7 = (bf16[128,3,3,64]{0,3,2,1:T(8,128)(2,1)}, bf16[128,3,3,64]{0,3,2,1:T(8,128)(2,1)S(1)}, u32[]{:S(2)}) copy-start(bf16[128,3,3,64]{0,3,2,1:T(8,128)(2,1)S(1)} %fusion.30) | copy-start | bytes 442372
  93.0 2.0 copy-start.15
  93.1 3.3 %copy-start.13 = (bf16[4,144,768]{2,1,0:T(8,128)(2,1)S(1)}, bf16[4,144,768]{2,1,0:T(8,128)(2,1)}, u32[]{:S(2)}) copy-start(bf16[4,144,768]{2,1,0:T(8,128)(2,1)} %get-tuple-element.41) | copy-start | bytes 2654212
  95.0 2.8 %copy-start.5 = (bf16[512,384]{0,1:T(8,128)(2,1)}, bf16[512,384]{0,1:T(8,128)(2,1)S(1)}, u32[]{:S(2)}) copy-start(bf16[512,384]{0,1:T(8,128)(2,1)S(1)} %get-tuple-element.105) | copy-start | bytes 1179652
  95.1 2.8 %copy-start.16 = (bf16[4,128,576]{2,1,0:T(8,128)(2,1)S(1)}, bf16[4,128,576]{2,1,0:T(8,128)(2,1)}, u32[]{:S(2)}) copy-start(bf16[4,128,576]{2,1,0:T(8,128)(2,1)} %get-tuple-element.40) | copy-start | bytes 1769476
  104.4 14.6 %copy-start.8 = (bf16[128,3,3,64]{0,3,2,1:T(8,128)(2,1)S(1)}, bf16[128,3,3,64]{0,3,2,1:T(8,128)(2,1)}, u32[]{:S(2)}) copy-start(bf16[128,3,3,64]{0,3,2,1:T(8,128)(2,1)} %copy-done.7) | copy-start | bytes 442372
  104.5 14.7 %copy-start.6 = (bf16[512,384]{0,1:T(8,128)(2,1)S(1)}, bf16[512,384]{0,1:T(8,128)(2,1)}, u32[]{:S(2)}) copy-start(bf16[512,384]{0,1:T(8,128)(2,1)} %copy-done.5) | copy-start | bytes 1179652
  118.7 3.7 %copy-start.10 = (pred[128,1024]{0,1:T(8,128)(4,1)S(1)}, pred[128,1024]{0,1:T(8,128)(4,1)}, u32[]{:S(2)}) copy-start(pred[128,1024]{0,1:T(8,128)(4,1)} %copy-done.9) | copy-start | bytes 393220
  122.4 4.4 %copy-start.19 = (bf16[1024,192]{0,1:T(8,128)(2,1)S(1)}, bf16[1024,192]{0,1:T(8,128)(2,1)}, u32[]{:S(2)}) copy-start(bf16[1024,192]{0,1:T(8,128)(2,1)} %copy-done.18) | copy-start | bytes 1179652
  130.6 0.9 copy-start.4
  136.1 23.0 %copy-start.1 = (bf16[4,144,960]{2,1,0:T(8,128)(2,1)S(1)}, bf16[4,144,960]{2,1,0:T(8,128)(2,1)}, u32[]{:S(2)}) copy-start(bf16[4,144,960]{2,1,0:T(8,128)(2,1)} %get-tuple-element.34) | copy-start | bytes 3317764
  159.7 4.4 %copy-start.12 = (bf16[4,144,768]{2,1,0:T(8,128)(2,1)S(1)}, bf16[4,144,768]{2,1,0:T(8,128)(2,1)}, u32[]{:S(2)}) copy-start(bf16[4,144,768]{2,1,0:T(8,128)(2,1)} %get-tuple-element.44) | copy-start | bytes 2654212
  192.4 20.8 %copy-start.17 = (bf16[4,432,128]{2,1,0:T(8,128)(2,1)S(1)}, bf16[4,432,128]{2,1,0:T(8,128)(2,1)}, u32[]{:S(2)}) copy-start(bf16[4,432,128]{2,1,0:T(8,128)(2,1)} %get-tuple-element.51) | copy-start | bytes 1327108
  208.5 3.5 %copy-start.20 = (bf16[4,216,128]{2,1,0:T(8,128)(2,1)S(1)}, bf16[4,216,128]{2,1,0:T(8,128)(2,1)}, u32[]{:S(2)}) copy-start(bf16[4,216,128]{2,1,0:T(8,128)(2,1)} %get-tuple-element.50) | copy-start | bytes 663556

commit v3 on v2

--- a/solution.py
+++ b/solution.py
@@ -307,13 +307,10 @@
     mat_out = mat_out.reshape(H * HD, D)
     ff_part = FF // dp_count
     d_part = D // dp_count
-    gate_up = jnp.concatenate(
-        [
-            slab.reshape(d_part, dp_count, ff_part)
-            for slab in unpack(got_gate_up, (w_gate.shape[0], w_up.shape[0]), (FF, FF))
-        ],
-        axis=2,
-    ).transpose(1, 0, 2)
+    gate_slab, up_slab = (
+        slab.reshape(d_part, dp_count, ff_part).transpose(1, 0, 2)
+        for slab in unpack(got_gate_up, (w_gate.shape[0], w_up.shape[0]), (FF, FF))
+    )
 
     inv_attn = lax.rsqrt(jnp.mean(row_input * row_input, axis=-1, keepdims=True) + norm_epsilon)
     normed_attn = (row_input * inv_attn * gain_attn).astype(low)
@@ -325,8 +322,8 @@
     packed_kv = jnp.concatenate(
         [turned[:, H:].reshape(span_rows, KV * HD), qkv[:, (H + KV) * HD :].astype(low)], axis=1
     )
-    all_kv, mat_gu = exchange(3, (packed_kv, "ctx", "gather"), (gate_up, "dp", "swap"))
-    mat_gu = mat_gu.reshape(D, 2 * ff_part)
+    all_kv, mat_gate = exchange(3, (packed_kv, "ctx", "gather"), (gate_slab, "dp", "swap"))
+    mat_gate = mat_gate.reshape(D, ff_part)
     all_kv = all_kv.reshape(seq_rows, 2 * KV * HD)
     all_keys = all_kv[:, : KV * HD].reshape(seq_rows, KV, HD)
     all_vals = all_kv[:, KV * HD :].reshape(seq_rows, KV, HD)
@@ -361,26 +358,33 @@
     inv_ffn = lax.rsqrt(jnp.mean(hidden * hidden, axis=-1, keepdims=True) + norm_epsilon)
     normed_ffn = (hidden * inv_ffn * gain_ffn).astype(low)
 
-    all_normed, got_down = exchange(
-        4, (normed_ffn, "dp", "gather"), (pack((w_down,)), "ctx", "gather")
-    )
+    all_normed, got_down, mat_up = exchange(
+        4,
+        (normed_ffn, "dp", "gather"),
+        (pack((w_down,)), "ctx", "gather"),
+        (up_slab, "dp", "swap"),
+    )
+    mat_up = mat_up.reshape(D, ff_part)
     (mat_down,) = unpack(got_down, (w_down.shape[0],), (D,))
     all_normed = all_normed.reshape(-1, D)
-    gate_up_act = matmul(all_normed, mat_gu)
-    gate = gate_up_act[:, :ff_part]
-    up_proj = gate_up_act[:, ff_part:]
+    gate = matmul(all_normed, mat_gate)
+    up_proj = matmul(all_normed, mat_up)
     sigma = jax.nn.sigmoid(gate)
     mixed = (gate * sigma * up_proj).astype(low)
     part_out = matmul(mixed, mat_down).astype(low).reshape(dp_count, span_rows, D)
     grad_mixed = matmul(all_cot, mat_down.T)
     grad_up = (grad_mixed * gate * sigma).astype(low)
     grad_gate = (grad_mixed * up_proj * sigma * (1.0 + gate * (1.0 - sigma))).astype(low)
-    grad_gu_act = jnp.concatenate([grad_gate, grad_up], axis=1)
-    part_normed = matmul(grad_gu_act, mat_gu.T).astype(low).reshape(dp_count, span_rows, D)
+    part_normed = matmul(grad_gate, mat_gate.T) + matmul(grad_up, mat_up.T)
+    part_normed = part_normed.astype(low).reshape(dp_count, span_rows, D)
     grad_down = matmul(mixed.T, all_cot).astype(low)
-    grad_gu = matmul(all_normed.T, grad_gu_act).astype(low).reshape(dp_count, d_part, -1)
-    got_normed, got_down_grad = exchange(
-        5, (part_normed, "dp", "sum"), (pack_grads((grad_down,), ctx_count), "ctx", "sum")
+    grad_mat_gate = matmul(all_normed.T, grad_gate).astype(low).reshape(dp_count, d_part, -1)
+    grad_mat_up = matmul(all_normed.T, grad_up).astype(low).reshape(dp_count, d_part, -1)
+    got_normed, got_down_grad, got_gate = exchange(
+        5,
+        (part_normed, "dp", "sum"),
+        (pack_grads((grad_down,), ctx_count), "ctx", "sum"),
+        (grad_mat_gate, "dp", "swap"),
     )
     grad_normed_ffn = total_of(got_normed)
 
@@ -430,9 +434,9 @@
             ).astype(low)
         )
     key_terms = jnp.concatenate(key_terms, axis=0).reshape(ctx_count, span_rows, 2 * KV * HD)
-    got_terms, got_gu = exchange(6, (key_terms, "ctx", "sum"), (grad_gu, "dp", "swap"))
-    slab_gate = got_gu[:, :, :ff_part].transpose(1, 0, 2).reshape(d_part, FF)
-    slab_up = got_gu[:, :, ff_part:].transpose(1, 0, 2).reshape(d_part, FF)
+    got_terms, got_up = exchange(6, (key_terms, "ctx", "sum"), (grad_mat_up, "dp", "swap"))
+    slab_gate = got_gate.transpose(1, 0, 2).reshape(d_part, FF)
+    slab_up = got_up.transpose(1, 0, 2).reshape(d_part, FF)
     own_grads = total_of(got_terms)
     grad_qk = rotate(
         jnp.concatenate(

time: 215 us -> 232 us (1.079)
  local copies, waits for them, and re-layouts: 26.2 us -> 33.4 us
  other arithmetic: 22.9 us -> 26.7 us
  matrix products: 27.1 us -> 30.7 us
  Pallas kernels: 136 us -> 139 us
    dot_general x12 -> x15, matrix products: 15.4 us -> 22.1 us  [matmul(): return jnp.dot(left, right, preferred_element_type=jnp.float32)]
    transpose x3 -> x2, local copies, waits for them, and re-layouts: 0.43 us -> 3.17 us  [the longest x1 1.99 us: on_device(): slab_gate = got_gate.transpose(1, 0, 2).reshape(d_part, FF)]
    pallas_call x8, Pallas kernels: 136 us -> 139 us  [exchange(): pl.pallas_call(kernel, out_shape=shapes, in_specs=[pl.BlockSpec(memory_sp...]
    unnamed x53 -> x65, local copies, waits for them, and re-layouts: 5.72 us -> 4.23 us
where the time goes in v3:
time: 232 us; the launch traced here: 231 us
  Pallas kernels  139 us (60%)
  local copies, waits for them, and re-layouts  33.4 us (14%)
  matrix products  30.7 us (13%)
  other arithmetic  26.7 us (12%)
    pallas_call x8, Pallas kernels, exchange(): pl.pallas_call(kernel, out_shape=shapes, in_specs=[pl.BlockSpec(memory_sp...  139 us
    dot_general x15, matrix products, matmul(): return jnp.dot(left, right, preferred_element_type=jnp.float32)  22.1 us
    reduce_sum x10, other arithmetic, total_of(): return jnp.sum(pieces.astype(jnp.float32), axis=0)  11.2 us

profile of v3, /device:TPU:0, one launch (start us, length us, event | category | flops | bytes accessed | tf_op | source)
XLA Modules:
  0.0 231.1 jit_solution(10745232393365847259)
XLA Ops:
  1.5 1.4 pad_maximum_fusion.12.refs_0_
  2.9 1.5 pad_maximum_fusion.10.refs_2_
  4.4 1.1 copy.98
  5.6 1.1 copy.99
  7.5 15.9 %shard_map.203 = (bf16[8,216,128]{2,1,0:T(8,128)(2,1)}, s32[8,1,128]{2,1,0:T(1,128)}, bf16[4,128,576]{2,1,0:T(8,128)(2,1)}) custom-call(bf16[216,128]{1,0:T(8,128)(2,1)} %pad_maximum_fusion.12.refs_0_, s32[1,128]{1,0:T(1,128)} %refs_1_.1, bf16[128,576]{1,0:T(8,128)(2,1)} %bitcast_convert_fusion.refs_2_), custom_call_target="tpu_custom_call" | custom-call | tf_op jit(solution)/shard_map/pallas_call | solution.py:201
  23.4 0.9 fusion.34
  24.3 1.0 fusion.57
  25.4 1.1 fusion.56
  26.4 0.9 reshape.355.refs_1_
  27.7 0.8 pad_maximum_fusion.3.refs_0_
  28.5 20.0 %shard_map.204 = (bf16[4,144,960]{2,1,0:T(8,128)(2,1)}, bf16[4,144,576]{2,1,0:T(8,128)(2,1)}, bf16[8,432,128]{2,1,0:T(8,128)(2,1)}) custom-call(bf16[144,960]{1,0:T(8,128)(2,1)} %pad_maximum_fusion.3.refs_0_, bf16[144,576]{1,0:T(8,128)(2,1)} %reshape.355.refs_1_, bf16[432,128]{1,0:T(8,128)(2,1)} %pad_maximum_fusion.10.refs_2_), custom_call_target="tpu_custom_call" | custom-call | tf_op jit(solution)/shard_map/pallas_call | solution.py:201
  48.6 2.0 fusion.41
  51.7 1.2 fusion.54
  53.2 0.8 copy.137
  54.2 0.8 copy.138
  55.1 17.8 %shard_map.205 = (bf16[8,128,384]{2,1,0:T(8,128)(2,1)}, bf16[4,144,384]{2,1,0:T(8,128)(2,1)}) custom-call(bf16[128,384]{1,0:T(8,128)(2,1)} %pad_maximum_fusion.11.refs_0_, bf16[4,144,384]{2,1,0:T(8,128)(2,1)} %bitcast.203), custom_call_target="tpu_custom_call" | custom-call | tf_op jit(solution)/shard_map/pallas_call | solution.py:201
  72.8 1.5 fusion.55
  74.7 0.9 fusion.5
  75.6 1.0 fusion.2
  77.2 1.2 fusion.31
  79.7 13.1 %shard_map.206 = (bf16[4,128,576]{2,1,0:T(8,128)(2,1)}, bf16[8,216,128]{2,1,0:T(8,128)(2,1)}, bf16[4,144,384]{2,1,0:T(8,128)(2,1)}) custom-call(bf16[128,576]{1,0:T(8,128)(2,1)} %multiply_convert_fusion.4.refs_0_, bf16[216,128]{1,0:T(8,128)(2,1)} %bitcast.231, bf16[4,144,384]{2,1,0:T(8,128)(2,1)} %bitcast.202), custom_call_target="tpu_custom_call" | custom-call | tf_op jit(solution)/shard_map/pallas_call | solution.py:201
  92.8 1.4 reshape.368
  94.2 1.6 fusion.59
  95.9 1.7 fusion.60
  97.6 2.9 %multiply_convert_fusion = (bf16[512,384]{1,0:T(8,128)(2,1)S(1)}, bf16[512,384]{1,0:T(8,128)(2,1)}, bf16[512,384]{1,0:T(8,128)(2,1)}) fusion(f32[512,384]{1,0:T(8,128)S(1)} %fusion.60, f32[512,384]{1,0:T(8,128)S(1)} %fusion.59, bf16[512,576]{1,0:T(8,128)(2,1)} %bitcast.214, bf16[576,384]{1,0:T(8,128)(2,1)} %bitcast.221), kind=kOutput, calls=%fused_computation.39 | convolution fusion | flops 229638144 | bytes 3784704 | tf_op jit(solution)/shard_map/dot_general | solution.py:20
  100.5 1.3 convolution_convert_fusion.5
  102.3 1.3 copy.109
  103.5 1.3 reshape_reshape.27.refs_1_
  104.9 1.3 copy.120
  106.2 2.5 %convolution_convert_fusion.4 = bf16[576,384]{1,0:T(8,128)(2,1)} fusion(bf16[512,576]{1,0:T(8,128)(2,1)} %bitcast.215, bf16[512,384]{1,0:T(8,128)(2,1)} %get-tuple-element.108), kind=kOutput, calls=%fused_computation.23 | convolution fusion | flops 226713600 | bytes 1425408 | tf_op jit(solution)/shard_map/dot_general | solution.py:20
  108.7 2.5 %convolution_convert_fusion.3 = bf16[576,384]{1,0:T(8,128)(2,1)} fusion(bf16[512,576]{1,0:T(8,128)(2,1)} %bitcast.216, bf16[512,384]{1,0:T(8,128)(2,1)} %get-tuple-element.109), kind=kOutput, calls=%fused_computation.22 | convolution fusion | flops 226713600 | bytes 1425408 | tf_op jit(solution)/shard_map/dot_general | solution.py:20
  111.2 1.5 fusion.61
  113.2 1.1 copy.108
  114.3 14.5 %shard_map.207 = (bf16[2,128,576]{2,1,0:T(8,128)(2,1)}, bf16[4,216,128]{2,1,0:T(8,128)(2,1)}, bf16[4,144,384]{2,1,0:T(8,128)(2,1)}) custom-call(bf16[2,2,128,576]{3,2,1,0:T(8,128)(2,1)} %bitcast.197, bf16[4,2,216,128]{3,2,1,0:T(8,128)(2,1)} %reshape_reshape.27.refs_1_, bf16[4,144,384]{2,1,0:T(8,128)(2,1)} %bitcast.223), custom_call_target="tpu_custom_call" | custom-call | tf_op jit(solution)/shard_map/pallas_call | solution.py:201
  128.8 1.1 convert_reduce_fusion.3
  129.9 2.0 copy.118
  131.9 2.0 concatenate.66
  134.1 0.9 bitcast_add_fusion
  135.4 1.9 convert_reduce_fusion.4
  137.3 3.6 %fusion.21 = bf16[1024,3,64]{0,2,1:T(8,128)(2,1)S(1)} fusion(bf16[128,3,3,64]{0,3,2,1:T(8,128)(2,1)S(1)} %bitcast.218, f32[3,1024,128,3]{2,1,3,0:T(8,128)} %copy-done, f32[3,3,128]{2,1,0:T(4,128)S(1)} %copy-done.26, pred[128,1024]{0,1:T(8,128)(4,1)} %copy-done.10), kind=kOutput, calls=%fused_computation.27 | convolution fusion | flops 155910144 | bytes 5394944 | tf_op jit(solution)/shard_map/kgqs,qkgd->skd/dot_general | solution.py:424
  140.9 1.5 fusion.1
  143.0 0.9 fusion.24
  143.9 1.1 concatenate.60
  145.8 1.4 copy.113
  147.1 1.2 pad_maximum_fusion.1.refs_0_
  148.3 19.8 %shard_map.208 = (bf16[4,128,384]{2,1,0:T(8,128)(2,1)}, bf16[4,144,384]{2,1,0:T(8,128)(2,1)}) custom-call(bf16[4,2,128,384]{3,2,1,0:T(8,128)(2,1)} %pad_maximum_fusion.1.refs_0_, bf16[4,144,384]{2,1,0:T(8,128)(2,1)} %bitcast.220), custom_call_target="tpu_custom_call" | custom-call | tf_op jit(solution)/shard_map/pallas_call | solution.py:201
  168.2 1.7 convert_reduce_fusion.1
  169.9 1.2 copy.119
  171.3 2.0 pad_maximum_fusion.refs_3_
  173.3 1.0 slice.167
  174.3 0.9 slice.124
  176.3 0.9 copy.123
  177.8 2.1 convolution_convert_fusion.1
  179.9 1.6 convolution_convert_fusion
  181.5 23.1 %shard_map.209 = (f32[4,2,576]{2,1,0:T(2,128)}, bf16[2,144,960]{2,1,0:T(8,128)(2,1)}, bf16[2,144,576]{2,1,0:T(8,128)(2,1)}, bf16[4,432,128]{2,1,0:T(8,128)(2,1)}) custom-call(f32[2,576]{1,0:T(2,128)} %pad_maximum_fusion.14.refs_0_, bf16[2,2,144,960]{3,2,1,0:T(8,128)(2,1)} %bitcast.188, bf16[2,2,144,576]{3,2,1,0:T(8,128)(2,1)} %bitcast.195, ...), custom_call_target="tpu_custom_call" | custom-call | tf_op jit(solution)/shard_map/pallas_call | solution.py:201
  204.6 1.4 reduce_sum.177.refs_0_
  206.0 1.1 reduce_sum.179
  207.1 1.2 reduce_sum.178
  209.2 0.9 pad_maximum_fusion.2.refs_2_
  210.1 14.7 %shard_map.210 = (f32[8,2,576]{2,1,0:T(2,128)}, bf16[2,128,576]{2,1,0:T(8,128)(2,1)}, bf16[4,216,128]{2,1,0:T(8,128)(2,1)}) custom-call(f32[2,576]{1,0:T(2,128)} %reduce_sum.177.refs_0_, bf16[2,2,128,576]{3,2,1,0:T(8,128)(2,1)} %bitcast.196, bf16[4,2,216,128]{3,2,1,0:T(8,128)(2,1)} %pad_maximum_fusion.2.refs_2_), custom_call_target="tpu_custom_call" | custom-call | tf_op jit(solution)/shard_map/pallas_call | solution.py:201
  224.7 1.1 convert_reduce_fusion.2
  225.9 0.9 copy.122
  226.7 0.8 reduce_sum.182
  228.1 1.0 convert_reduce_fusion.5
  (118 shorter events, 14.2 us)
Async XLA Ops:
  0.6 47.9 %copy-start.21 = (f32[576]{0:T(1024)S(1)}, f32[576]{0:T(1024)}, u32[]{:S(2)}) copy-start(f32[576]{0:T(1024)} %param.14) | copy-start | bytes 6916
  0.7 47.9 %copy-start.12 = (f32[1,128,576]{1,2,0:T(8,128)S(1)}, f32[1,128,576]{1,2,0:T(8,128)}, u32[]{:S(2)}) copy-start(f32[1,128,576]{1,2,0:T(8,128)} %param.12) | copy-start | bytes 884740
  1.5 49.2 %copy-start.18 = (f32[128,32]{0,1:T(8,128)}, f32[128,32]{0,1:T(8,128)S(1)}, u32[]{:S(2)}) copy-start(f32[128,32]{0,1:T(8,128)S(1)} %get-tuple-element.132) | copy-start | bytes 49156
  5.6 47.3 %copy-start.24 = (f32[128]{0:T(128)}, f32[128]{0:T(128)S(1)}, u32[]{:S(2)}) copy-start(f32[128]{0:T(128)S(1)} %add_rsqrt_fusion.1) | copy-start | bytes 1540
  24.3 52.9 %copy-start.10 = (pred[128,1024]{0,1:T(8,128)(4,1)}, pred[128,1024]{0,1:T(8,128)(4,1)S(1)}, u32[]{:S(2)}) copy-start(pred[128,1024]{0,1:T(8,128)(4,1)S(1)} %fusion.34) | copy-start | bytes 393220
  50.8 23.9 %copy-start.6 = (bf16[128,9,64]{0,2,1:T(8,128)(2,1)}, bf16[128,9,64]{0,2,1:T(8,128)(2,1)S(1)}, u32[]{:S(2)}) copy-start(bf16[128,9,64]{0,2,1:T(8,128)(2,1)S(1)} %pad_maximum_fusion.9) | copy-start | bytes 442372
  74.7 2.5 %copy-start.15 = (bf16[1024,192]{0,1:T(8,128)(2,1)}, bf16[1024,192]{0,1:T(8,128)(2,1)S(1)}, u32[]{:S(2)}) copy-start(bf16[1024,192]{0,1:T(8,128)(2,1)S(1)} %copy.104) | copy-start | bytes 1179652
  75.6 2.9 %copy-start = (f32[3,1024,128,3]{2,1,3,0:T(8,128)}, f32[3,1024,128,3]{2,1,3,0:T(8,128)S(1)}, u32[]{:S(2)}) copy-start(f32[3,1024,128,3]{2,1,3,0:T(8,128)S(1)} %get-tuple-element.134) | copy-start | bytes 14155780
  76.6 1.9 copy-start.2
  76.6 2.4 %copy-start.23 = (f32[576]{0:T(1024)S(1)}, f32[576]{0:T(1024)}, u32[]{:S(2)}) copy-start(f32[576]{0:T(1024)} %param.15) | copy-start | bytes 6916
  78.5 22.0 %copy-start.8 = (bf16[128,3,3,64]{0,3,2,1:T(8,128)(2,1)}, bf16[128,3,3,64]{0,3,2,1:T(8,128)(2,1)S(1)}, u32[]{:S(2)}) copy-start(bf16[128,3,3,64]{0,3,2,1:T(8,128)(2,1)S(1)} %fusion.31) | copy-start | bytes 442372
  78.5 17.4 %copy-start.4 = (bf16[4,144,384]{2,1,0:T(8,128)(2,1)S(1)}, bf16[4,144,384]{2,1,0:T(8,128)(2,1)}, u32[]{:S(2)}) copy-start(bf16[4,144,384]{2,1,0:T(8,128)(2,1)} %get-tuple-element.44) | copy-start | bytes 1327108
  79.0 54.9 %copy-start.27 = (f32[128]{0:T(128)}, f32[128]{0:T(128)S(1)}, u32[]{:S(2)}) copy-start(f32[128]{0:T(128)S(1)} %add_rsqrt_fusion) | copy-start | bytes 1540
  95.9 4.6 %copy-start.3 = (bf16[4,128,576]{2,1,0:T(8,128)(2,1)S(1)}, bf16[4,128,576]{2,1,0:T(8,128)(2,1)}, u32[]{:S(2)}) copy-start(bf16[4,128,576]{2,1,0:T(8,128)(2,1)} %get-tuple-element.40) | copy-start | bytes 1769476
  104.9 6.3 %copy-start.5 = (bf16[4,144,384]{2,1,0:T(8,128)(2,1)S(1)}, bf16[4,144,384]{2,1,0:T(8,128)(2,1)}, u32[]{:S(2)}) copy-start(bf16[4,144,384]{2,1,0:T(8,128)(2,1)} %get-tuple-element.44) | copy-start | bytes 1327108
  106.2 6.5 %copy-start.13 = (bf16[4,144,384]{2,1,0:T(8,128)(2,1)S(1)}, bf16[4,144,384]{2,1,0:T(8,128)(2,1)}, u32[]{:S(2)}) copy-start(bf16[4,144,384]{2,1,0:T(8,128)(2,1)} %get-tuple-element.43) | copy-start | bytes 1327108
  106.2 6.5 %copy-start.17 = (bf16[512,384]{1,0:T(8,128)(2,1)S(1)}, bf16[512,384]{1,0:T(8,128)(2,1)}, u32[]{:S(2)}) copy-start(bf16[512,384]{1,0:T(8,128)(2,1)} %get-tuple-element.109) | copy-start | bytes 1179652
  114.3 21.0 %copy-start.9 = (bf16[128,3,3,64]{0,3,2,1:T(8,128)(2,1)S(1)}, bf16[128,3,3,64]{0,3,2,1:T(8,128)(2,1)}, u32[]{:S(2)}) copy-start(bf16[128,3,3,64]{0,3,2,1:T(8,128)(2,1)} %copy-done.8) | copy-start | bytes 442372
  114.3 22.9 %copy-start.26 = (f32[3,3,128]{2,1,0:T(4,128)S(1)}, f32[3,3,128]{2,1,0:T(4,128)}, u32[]{:S(2)}) copy-start(f32[3,3,128]{2,1,0:T(4,128)} %log_add_fusion) | copy-start | bytes 13828
  114.3 26.5 %slice-start = ((s8[4718592]{0:T(1024)(128)(4,1)}), s8[524288]{0:T(1024)(128)(4,1)S(1)}, s32[]{:S(2)}) async-start(s8[4718592]{0:T(1024)(128)(4,1)} %bitcast.186), calls=%async_computation | async-start | bytes 1048576
  134.1 6.8 %copy-start.11 = (pred[128,1024]{0,1:T(8,128)(4,1)S(1)}, pred[128,1024]{0,1:T(8,128)(4,1)}, u32[]{:S(2)}) copy-start(pred[128,1024]{0,1:T(8,128)(4,1)} %copy-done.10) | copy-start | bytes 393220
  134.1 6.8 %copy-start.16 = (bf16[1024,192]{0,1:T(8,128)(2,1)S(1)}, bf16[1024,192]{0,1:T(8,128)(2,1)}, u32[]{:S(2)}) copy-start(bf16[1024,192]{0,1:T(8,128)(2,1)} %copy-done.15) | copy-start | bytes 1179652
  135.0 5.9 %slice-start.1 = ((s8[4718592]{0:T(1024)(128)(4,1)}), s8[4194304]{0:T(1024)(128)(4,1)S(1)}, s32[]{:S(2)}) async-start(s8[4718592]{0:T(1024)(128)(4,1)} %bitcast.186), calls=%async_computation.1 | async-start | bytes 8388608
  140.9 2.1 copy-start.7
  145.2 30.2 %copy-start.19 = (f32[128,32]{0,1:T(8,128)S(1)}, f32[128,32]{0,1:T(8,128)}, u32[]{:S(2)}) copy-start(f32[128,32]{0,1:T(8,128)} %copy-done.18) | copy-start | bytes 49156
  145.2 30.2 %copy-start.20 = (f32[128,32]{0,1:T(8,128)S(1)}, f32[128,32]{0,1:T(8,128)}, u32[]{:S(2)}) copy-start(f32[128,32]{0,1:T(8,128)} %get-tuple-element.130) | copy-start | bytes 49156
  145.7 29.8 %copy-start.1 = (bf16[4,144,960]{2,1,0:T(8,128)(2,1)S(1)}, bf16[4,144,960]{2,1,0:T(8,128)(2,1)}, u32[]{:S(2)}) copy-start(bf16[4,144,960]{2,1,0:T(8,128)(2,1)} %get-tuple-element.36) | copy-start | bytes 3317764
  145.7 29.8 %copy-start.22 = (f32[576]{0:T(1024)S(1)}, f32[576]{0:T(1024)}, u32[]{:S(2)}) copy-start(f32[576]{0:T(1024)} %param.14) | copy-start | bytes 6916
  145.7 29.8 %copy-start.25 = (f32[128]{0:T(128)S(1)}, f32[128]{0:T(128)}, u32[]{:S(2)}) copy-start(f32[128]{0:T(128)} %copy-done.24) | copy-start | bytes 1540
  204.6 25.8 %copy-start.14 = (bf16[4,432,128]{2,1,0:T(8,128)(2,1)S(1)}, bf16[4,432,128]{2,1,0:T(8,128)(2,1)}, u32[]{:S(2)}) copy-start(bf16[4,432,128]{2,1,0:T(8,128)(2,1)} %get-tuple-element.55) | copy-start | bytes 1327108
